TPU v7x, 256 devices: a whole 4x4x8 slice. The times are simulated.
256 devices in a mesh: dp: 32 (over y, z), order: 8 (over x, core).
Axes of the slice: x: 4, y: 4, z: 8, core: 2. Of those that a mesh axis runs over, the one named last changes fastest.
Arguments:
- images: bfloat16 [8192, 128, 512], P(('dp', 'order')), may hold values from -6 to 6
- radial_interp: bfloat16 [128, 128], replicated, may hold values from -0.5 to 0.5
- assignment: int32 [256], replicated, may hold values from 0 to 255, as said below
- counts: int32 [256], P('order'), may hold values from 32 to 128, as said below
- radial_basis: bfloat16 [256, 128, 128], P('order'), may hold values from -0.5 to 0.5
- eigenbasis: bfloat16 [256, 128, 128], P('order'), may hold values from -0.5 to 0.5
Outputs:
- covariance: float32 [256, 32768], P(('order', 'dp'))
- projected: bfloat16 [2, 256, 8192, 128], P(None, 'order', 'dp')
Inputs may be any that keep to these rules, and one draw needn't show every extreme that they name: `assignment`: a permutation of the orders 0 to 255. The slot of order 0 keeps 128; the slot of order 256 - 1 keeps 32; counts fall with the order up to a jitter of 3.
All inputs are finite; a program needn't handle non-finite values.
Results may differ from a plain program's by a relative error of at most 0.013.
Values may be sent and summed in bfloat16 or wider, within the bound.
No kernel may reach another device: no remote copies, remote signals or barrier semaphores. Data moves between devices by JAX's collectives and lax.ppermute only.
A program may use at most 128 MiB of HBM per device.

v0:
```python
import math

import jax
import jax.numpy as jnp
from jax import lax
from jax.sharding import PartitionSpec as P


def build_table(slot_orders, samples):
    angle_index = jnp.arange(samples, dtype=jnp.int32)[:, None]
    product = angle_index * slot_orders[None, :] % samples
    theta = product.astype(jnp.float32) * (2.0 * math.pi / samples)
    factor = 1.0 / math.sqrt(samples)
    return (jnp.concatenate([jnp.cos(theta), -jnp.sin(theta)], axis=1) * factor).astype(
        jnp.bfloat16
    )


def body(images, radial_interp, assignment, counts, radial_basis, eigenbasis):
    local_images = images.shape[0]
    samples = images.shape[2]
    nodes = radial_interp.shape[1]
    slot_total = assignment.shape[0]
    basis_width = radial_basis.shape[2]
    polar_grid = jnp.einsum(
        "isa,sr->ira", images, radial_interp, preferred_element_type=jnp.float32
    ).astype(jnp.bfloat16)
    dft_table = build_table(assignment, samples)
    spectrum = jnp.einsum(
        "ira,ac->cir", polar_grid, dft_table, preferred_element_type=jnp.float32
    ).astype(jnp.bfloat16)
    spectrum = spectrum.reshape(2, slot_total, local_images, nodes)
    owned_spec = lax.all_to_all(spectrum, "order", split_axis=1, concat_axis=2, tiled=True)
    kept_mask = (jnp.arange(basis_width, dtype=jnp.int32)[None, :] < counts[:, None]).astype(
        jnp.bfloat16
    )
    kept_basis = radial_basis * kept_mask[:, None, :]
    coefficients = jnp.einsum(
        "pkir,krj->pkij", owned_spec, kept_basis, preferred_element_type=jnp.float32
    ).astype(jnp.bfloat16)
    real_cov = jnp.einsum(
        "pkij,pkil->kjl", coefficients, coefficients, preferred_element_type=jnp.float32
    )
    imag_cov = jnp.einsum(
        "kij,kil->kjl", coefficients[1], coefficients[0], preferred_element_type=jnp.float32
    ) - jnp.einsum(
        "kij,kil->kjl", coefficients[0], coefficients[1], preferred_element_type=jnp.float32
    )
    owned_slots = coefficients.shape[1]
    image_total = coefficients.shape[2] * lax.axis_size("dp")
    partial_cov = (
        jnp.stack([real_cov, imag_cov], 1).reshape(owned_slots, 2 * basis_width * basis_width)
        / image_total
    )
    covariance = lax.psum_scatter(
        partial_cov.astype(jnp.bfloat16), "dp", scatter_dimension=0, tiled=True
    ).astype(jnp.float32)
    projected = jnp.einsum(
        "pkij,kje->pkie", coefficients, eigenbasis, preferred_element_type=jnp.float32
    ).astype(jnp.bfloat16)
    return (covariance, projected)


def solution(mesh):
    placed = (
        P(("dp", "order"), None, None),
        P(),
        P(),
        P("order"),
        P("order", None, None),
        P("order", None, None),
    )
    return jax.shard_map(
        body,
        mesh=mesh,
        in_specs=placed,
        out_specs=(P(("order", "dp"), None), P(None, "order", "dp", None)),
        check_vma=False,
    )
```

profile of v0, /device:TPU:24, one launch (start us, length us, event | category | flops | bytes accessed | tf_op | source)
XLA Modules:
  0.0 253.1 jit_solution(2026984075722020948)
XLA Ops:
  7.2 0.0 copy-start
  7.2 2.9 %fusion.25 = (f32[512,256]{0,1:T(8,128)S(1)}, f32[512,256]{0,1:T(8,128)S(1)}) fusion(s32[256]{0:T(256)} %param.8), kind=kLoop, calls=%fused_computation.34 | loop fusion | flops 1966080 | bytes 1049600 | tf_op jit(solution)/shard_map/cos | solution.py:14
  10.1 6.7 %fusion.6 = bf16[512,32,128]{2,0,1:T(8,128)(2,1)} fusion(bf16[32,128,512]{2,1,0:T(8,128)(2,1)} %param.6, f32[512,256]{0,1:T(8,128)S(1)} %get-tuple-element.9, f32[512,256]{0,1:T(8,128)S(1)} %get-tuple-element.8, bf16[128,128]{1,0:T(8,128)(2,1)} %param.7), kind=kOutput, calls=%fused_computation.8 | convolution fusion | flops 2689335296 | bytes 9469952 | tf_op jit(solution)/shard_map/ira,ac->cir/dot_general | solution.py:29
  16.8 8.5 %copy.24 = bf16[2,256,32,128]{3,0,2,1:T(2,128)(2,1)} copy(bf16[2,256,32,128]{3,1,0,2:T(8,128)(2,1)} %bitcast.63) | data formatting | bytes 8388608 | tf_op jit(solution)/shard_map/reshape | solution.py:32
  25.3 0.0 copy-start.3
  25.3 4.7 %all-to-all-start = ((bf16[2,256,32,128]{3,0,2,1:T(2,128)(2,1)}), bf16[2,256,32,128]{3,0,2,1:T(2,128)(2,1)}, u32[]{:S(2)}, u32[]{:S(2)}) async-start(bf16[2,256,32,128]{3,0,2,1:T(2,128)(2,1)} %copy.24), calls=%async_computation | async-start | bytes 8388608 | tf_op jit(solution)/shard_map/all_to_all | solution.py:33
  30.0 0.2 all-reduce.3.cloned.1.call-start
  30.2 0.0 copy-done.3
  30.2 0.1 fusion.28
  30.3 49.4 %all-to-all-done = bf16[2,256,32,128]{3,0,2,1:T(2,128)(2,1)} async-done(((bf16[2,256,32,128]{3,0,2,1:T(2,128)(2,1)}), bf16[2,256,32,128]{3,0,2,1:T(2,128)(2,1)}, u32[]{:S(2)}, u32[]{:S(2)}) %all-to-all-start) | async-done | bytes 4194336 | tf_op jit(solution)/shard_map/all_to_all | solution.py:33
  79.7 0.0 copy-start.2
  79.7 3.3 %copy.25 = bf16[2,8,32,32,128]{4,3,1,0,2:T(8,128)(2,1)S(1)} copy(bf16[2,8,32,32,128]{4,0,3,2,1:T(2,128)(2,1)} %bitcast.5) | data formatting | bytes 8388608 | tf_op jit(solution)/shard_map/all_to_all | solution.py:33
  83.0 0.0 copy-done.2
  83.0 1.3 convert_bitcast_fusion.1
  84.3 0.0 copy-start.1
  84.4 0.7 fusion.9
  85.1 1.2 convolution_bitcast_fusion
  86.3 0.0 copy-done.1
  86.4 0.8 subtract_bitcast_fusion
  87.1 0.5 fusion
  87.6 0.1 copy.30
  87.8 0.0 copy-start.4
  87.8 2.7 %copy.46 = bf16[4,8,256,128]{3,1,2,0:T(8,128)(2,1)} copy(bf16[4,8,256,128]{3,2,1,0:T(8,128)(2,1)S(1)} %bitcast.62) | data formatting | bytes 4194304
  90.5 0.0 all-reduce.3.cloned.1.call-update
  90.5 0.0 copy-done.4
  90.5 0.6 dynamic-slice
  91.1 0.0 copy-done
  91.1 3.5 %convert_bitcast_fusion = bf16[2,32,256,128]{3,2,0,1:T(8,128)(2,1)S(1)} fusion(bf16[2,32,256,128]{2,3,0,1:T(8,128)(2,1)} %copy-done.1, bf16[32,128,128]{2,1,0:T(8,128)(2,1)S(1)} %copy-done), kind=kOutput, calls=%fused_computation.4 | convolution fusion | flops 538968064 | bytes 9437184 | tf_op jit(solution)/shard_map/pkij,kje->pkie/dot_general | solution.py:58
  94.6 2.3 copy.32
  96.9 146.9 %all-reduce.3.cloned.1.call-done = bf16[32,32768]{1,0:T(8,128)(2,1)} async-done(((bf16[32,32768]{1,0:T(8,128)(2,1)}), bf16[32,32768]{1,0:T(8,128)(2,1)}) %all-reduce.3.cloned.1.call-update) | async-done | bytes 2097168
  243.8 2.4 dynamic-slice_convert_fusion
Async XLA Ops:
  7.2 83.9 %copy-start = (bf16[32,128,128]{2,1,0:T(8,128)(2,1)S(1)}, bf16[32,128,128]{2,1,0:T(8,128)(2,1)}, u32[]{:S(2)}) copy-start(bf16[32,128,128]{2,1,0:T(8,128)(2,1)} %param.11) | copy-start | bytes 3145732
  25.3 4.9 %copy-start.3 = (s32[32]{0:T(128)S(1)}, s32[32]{0:T(128)}, u32[]{:S(2)}) copy-start(s32[32]{0:T(128)} %param.9) | copy-start | bytes 388
  25.3 54.4 %all-to-all-start = ((bf16[2,256,32,128]{3,0,2,1:T(2,128)(2,1)}), bf16[2,256,32,128]{3,0,2,1:T(2,128)(2,1)}, u32[]{:S(2)}, u32[]{:S(2)}) async-start(bf16[2,256,32,128]{3,0,2,1:T(2,128)(2,1)} %copy.24), calls=%async_computation | async-start | bytes 8388608 | tf_op jit(solution)/shard_map/all_to_all | solution.py:33
  30.0 213.8 %all-reduce.3.cloned.1.call-start = ((), (), s32[]{:S(2)}) async-start(), calls=%async_computation.1 | async-start | bytes 4194304
  79.7 3.4 %copy-start.2 = (bf16[32,128,128]{2,1,0:T(8,128)(2,1)S(1)}, bf16[32,128,128]{2,1,0:T(8,128)(2,1)}, u32[]{:S(2)}) copy-start(bf16[32,128,128]{2,1,0:T(8,128)(2,1)} %param.10) | copy-start | bytes 3145732
  84.3 2.0 copy-start.1
  87.8 2.7 %copy-start.4 = (u32[256]{0:T(256)S(1)}, u32[256]{0:T(256)}, u32[]{:S(2)}) copy-start(u32[256]{0:T(256)} %constant.25) | copy-start | bytes 3076
Sparse Core Ops, SparseCore 0:
  90.6 153.1 all-reduce.2
where the time goes:
time: 256 us; the launch traced here: 253 us
  waiting for transfers between devices  196 us (77%)
  local copies, waits for them, and re-layouts  17.6 us (7%)
  matrix products  14.2 us (6%)
  between operations  14.1 us (6%)
  other arithmetic  5.92 us (2%)
  starting transfers between devices  4.91 us (2%)
    unnamed x2, waiting for transfers between devices  147 us
    all_to_all x1, waiting for transfers between devices, body(): lax.all_to_all(spectrum, 'order', split_axis=1, concat_axis=2, tiled=True)  49.4 us
    reshape x1, local copies, waits for them, and re-layouts, body(): spectrum = spectrum.reshape(2, slot_total, local_images, nodes)  8.48 us
    dot_general x1, matrix products, body(): jnp.einsum('ira,ac->cir', polar_grid, dft_table, preferred_element_type=j...  6.72 us
    unnamed x13, local copies, waits for them, and re-layouts  5.61 us
  transfers between devices with their start and end apart: 2, of which 2 were waited for; matrix products, arithmetic and copies ran while one was open for 3% of the time, Pallas kernels for 0%

commit v1 on v0

v1 whole, which is shorter than its diff:
```python
import functools
import math

import numpy as np
import jax
import jax.numpy as jnp
from jax import lax
from jax.experimental import pallas as pl
from jax.experimental.pallas import tpu as pltpu
from jax.sharding import PartitionSpec as P

NY, NZ = 4, 8
NO = 8
GROUPS = 4
FIRST = 3
EXCHANGE = (4, 5, 2, 6, 3, 7, 1)


def angle_tables(samples, orders):
    product = np.arange(orders)[:, None] * np.arange(samples)[None, :] % samples
    theta = product * (2.0 * math.pi / samples)
    factor = 1.0 / math.sqrt(samples)
    both = np.stack([np.cos(theta), -np.sin(theta)]) * factor
    return both.astype(np.float32).astype(jnp.bfloat16)


def spectrum_kernel(x_ref, interp_ref, slots_ref, tables_ref, *rest):
    outs, table = rest[:-1], rest[-1]
    total = tables_ref.shape[1]
    split = total * FIRST // GROUPS

    @pl.when(pl.program_id(0) == 0)
    def _():
        me = lax.axis_index("order")
        y = lax.axis_index("dp") // NZ
        row = lax.broadcasted_iota(jnp.int32, (2 * total, total), 0)
        part, s = row & 1, row >> 1
        late = s >= split
        t = jnp.where(late, s - split, s)
        per = FIRST * 8
        d_first = (t * 2731) >> 16
        d = jnp.where(late, t >> 3, d_first)
        g = jnp.where(late, FIRST, (t - d_first * per) >> 3)
        dy, zl = (t >> 1) & 3, t & 1
        slot = (me ^ d) * (NY * NZ) + (y ^ dy) * NZ + g * 2 + zl
        lane = lax.broadcasted_iota(jnp.int32, (2 * total, total), 1)
        pick = (slot == lane).astype(jnp.bfloat16)
        order = lax.broadcasted_iota(jnp.int32, (total, total), 0)
        holds = (slots_ref[...] == order).astype(jnp.bfloat16)
        hot = lax.dot_general(
            pick, holds, (((1,), (1,)), ((), ())), preferred_element_type=jnp.float32
        ).astype(jnp.bfloat16)
        cosine = jnp.dot(hot, tables_ref[0], preferred_element_type=jnp.float32)
        sine = jnp.dot(hot, tables_ref[1], preferred_element_type=jnp.float32)
        odd = lax.broadcasted_iota(jnp.int32, cosine.shape, 0) & 1
        table[...] = jnp.where(odd == 1, sine, cosine).astype(jnp.bfloat16)

    n = x_ref.shape[0]
    interp = interp_ref[...]
    nodes = interp.shape[1]
    for i in range(0, n, 2):
        polar = jnp.concatenate(
            [
                lax.dot_general(
                    interp, x_ref[i + h], (((0,), (0,)), ((), ())),
                    preferred_element_type=jnp.float32,
                ).astype(jnp.bfloat16)
                for h in range(2)
            ],
            axis=0,
        )
        spec = lax.dot_general(
            table[...], polar, (((1,), (1,)), ((), ())), preferred_element_type=jnp.float32
        ).astype(jnp.bfloat16)
        base = 0
        for out in outs:
            rows = out.shape[1]
            for h in range(2):
                out[i + h] = spec[base : base + rows, h * nodes : (h + 1) * nodes]
            base += rows


def spectra(images, interp, assignment):
    count, radii, samples = images.shape
    nodes = interp.shape[1]
    total = assignment.shape[0]
    step = 4
    heights = [2 * total * FIRST // GROUPS // NO] * NO
    heights += [2 * total * (GROUPS - FIRST) // GROUPS // NO] * NO
    tables = jnp.asarray(angle_tables(samples, total))
    return pl.pallas_call(
        spectrum_kernel,
        grid=(count // step,),
        in_specs=[
            pl.BlockSpec((step, radii, samples), lambda i: (i, 0, 0)),
            pl.BlockSpec((radii, nodes), lambda i: (0, 0)),
            pl.BlockSpec((1, total), lambda i: (0, 0)),
            pl.BlockSpec((2, total, samples), lambda i: (0, 0, 0)),
        ],
        out_specs=[pl.BlockSpec((step, h, nodes), lambda i: (i, 0, 0)) for h in heights],
        out_shape=[jax.ShapeDtypeStruct((count, h, nodes), jnp.bfloat16) for h in heights],
        scratch_shapes=[pltpu.VMEM((2 * total, samples), jnp.bfloat16)],
        compiler_params=pltpu.CompilerParams(vmem_limit_bytes=48 << 20),
        cost_estimate=pl.CostEstimate(
            flops=2 * count * nodes * samples * (radii + 2 * total),
            bytes_accessed=4 * count * radii * samples,
            transcendentals=0,
        ),
        name="spectra",
    )(images, interp, assignment[None, :], tables)


def slot_kernel(scale, start, aliased, counts_ref, *refs):
    pieces, (basis_ref, eigen_ref) = refs[:NO], refs[NO : NO + 2]
    rest = refs[NO + 2 + aliased :]
    out_ref, covs, wide = rest[0], rest[1 : 1 + NY], rest[-1]
    me = lax.axis_index("order")
    y = lax.axis_index("dp") // NZ
    group = start + pl.program_id(0)
    images, rows, nodes = pieces[0].shape
    for d in range(NO):
        wide[d] = pieces[d][...].astype(jnp.float32).reshape(images * rows, nodes)
    width = basis_ref.shape[3]
    lane = lax.broadcasted_iota(jnp.int32, (nodes, width), 1)
    row = lax.broadcasted_iota(jnp.int32, (width, width), 0)
    col = lax.broadcasted_iota(jnp.int32, (width, width), 1)
    upper = row <= col
    for dy in range(NY):
        yy = y ^ dy
        for zl in range(2):
            limit = counts_ref[yy * NZ + group * 2 + zl]
            basis = jnp.where(lane < limit, basis_ref[yy, zl], 0)
            spec = jnp.concatenate(
                [
                    wide[me ^ j, pl.ds(dy * 4 + zl * 2 + p, images, stride=rows), :]
                    for p in range(2)
                    for j in range(NO)
                ],
                axis=0,
            ).astype(jnp.bfloat16)
            coef = jnp.dot(spec, basis, preferred_element_type=jnp.float32).astype(jnp.bfloat16)
            half = coef.shape[0] // 2
            pair = jnp.concatenate([coef[:half], coef[half:]], axis=1)
            gram = lax.dot_general(
                pair, pair, (((0,), (0,)), ((), ())), preferred_element_type=jnp.float32
            )
            real = gram[:width, :width] + gram[width:, width:]
            imag = gram[width:, :width] - gram[:width, width:]
            covs[dy][zl] = (jnp.where(upper, real, imag) * scale).astype(jnp.bfloat16)
            projected = jnp.dot(
                coef, eigen_ref[yy, zl], preferred_element_type=jnp.float32
            ).astype(jnp.bfloat16)
            out_ref[0, yy, zl] = projected[:half]
            out_ref[1, yy, zl] = projected[half:]


def slots(pieces, counts, basis, eigen, scale, start, groups, earlier=None):
    images, _, nodes = pieces[0].shape
    owned, _, width = basis.shape
    ends = eigen.shape[2]
    rows = 4 * NY
    total = NO * images
    aliased = 0 if earlier is None else 1
    block = pl.BlockSpec((images, rows, nodes), lambda g, c: (0, g, 0))
    weights = pl.BlockSpec((NY, 2, nodes, width), lambda g, c: (0, start + g, 0, 0))
    in_specs = [block] * NO + [weights, weights]
    args = list(pieces) + [basis.reshape(NY, NZ, nodes, width), eigen.reshape(NY, NZ, width, ends)]
    if aliased:
        in_specs.append(pl.BlockSpec(memory_space=pl.ANY))
        args.append(earlier)
    return pl.pallas_call(
        functools.partial(slot_kernel, scale, start, aliased),
        grid_spec=pltpu.PrefetchScalarGridSpec(
            num_scalar_prefetch=1,
            grid=(groups,),
            in_specs=in_specs,
            out_specs=[
                pl.BlockSpec((2, NY, 2, total, ends), lambda g, c: (0, 0, start + g, 0, 0))
            ]
            + [pl.BlockSpec((2, width, width), lambda g, c: (g, 0, 0))] * NY,
            scratch_shapes=[pltpu.VMEM((NO, images * rows, nodes), jnp.float32)],
        ),
        out_shape=[jax.ShapeDtypeStruct((2, NY, NZ, total, ends), jnp.bfloat16)]
        + [jax.ShapeDtypeStruct((2 * groups, width, width), jnp.bfloat16)] * NY,
        input_output_aliases={len(args): 0} if aliased else {},
        compiler_params=pltpu.CompilerParams(vmem_limit_bytes=48 << 20),
        cost_estimate=pl.CostEstimate(
            flops=groups * 8 * 8 * total * nodes * width,
            bytes_accessed=groups * 4 << 20,
            transcendentals=0,
        ),
        name="slots",
    )(counts, *args)


def finish_kernel(parts_ref, out_ref):
    packed = parts_ref[0].astype(jnp.float32)
    for i in range(1, parts_ref.shape[0]):
        packed += parts_ref[i].astype(jnp.float32)
    other = packed.T
    row = lax.broadcasted_iota(jnp.int32, packed.shape, 0)
    col = lax.broadcasted_iota(jnp.int32, packed.shape, 1)
    out_ref[0] = jnp.where(row <= col, packed, other)
    out_ref[1] = jnp.where(row > col, packed, jnp.where(row < col, -other, 0.0))


def body(images, radial_interp, assignment, counts, radial_basis, eigenbasis):
    owned = radial_basis.shape[0]
    width = radial_basis.shape[2]
    total = images.shape[0] * lax.axis_size("order") * lax.axis_size("dp")
    pieces = spectra(images, radial_interp, assignment)

    def exchange(own):
        got = {0: own[0]}
        for d in EXCHANGE:
            got[d] = lax.ppermute(own[d], "order", [(i, i ^ d) for i in range(NO)])
        return [got[d] for d in range(NO)]

    def gather_y(covs):
        moved = [covs[0]]
        for dy in (2, 1, 3):
            perm = [(i, i ^ (dy * NZ)) for i in range(NY * NZ)]
            moved.append(lax.ppermute(covs[dy], "dp", perm))
        return sum(m.astype(jnp.float32) for m in moved).astype(jnp.bfloat16)

    first = exchange(pieces[:NO])
    second = exchange(pieces[NO:])
    scale = 1.0 / total
    projected, *cov_first = slots(
        first, counts, radial_basis, eigenbasis, scale, 0, FIRST
    )
    sum_first = gather_y(cov_first)
    projected, *cov_second = slots(
        second, counts, radial_basis, eigenbasis, scale, FIRST, GROUPS - FIRST, projected
    )
    sum_second = gather_y(cov_second)
    parts = jnp.concatenate([sum_first, sum_second], axis=0)
    rings = [[y * NZ + z for z in range(NZ)] for y in range(NY)]
    parts = lax.all_to_all(parts, "dp", 0, 0, axis_index_groups=rings, tiled=True)
    covariance = pl.pallas_call(
        finish_kernel,
        out_shape=jax.ShapeDtypeStruct((2, width, width), jnp.float32),
        name="finish",
    )(parts)
    projected = projected.reshape(2, owned, projected.shape[3], projected.shape[4])
    return (covariance.reshape(1, 2 * width * width), projected)


def solution(mesh):
    placed = (
        P(("dp", "order"), None, None),
        P(),
        P(),
        P("order"),
        P("order", None, None),
        P("order", None, None),
    )
    return jax.shard_map(
        body,
        mesh=mesh,
        in_specs=placed,
        out_specs=(P(("order", "dp"), None), P(None, "order", "dp", None)),
        check_vma=False,
    )
```

time: 256 us -> 127 us (0.50)
  waiting for transfers between devices: 196 us -> 52.8 us
  Pallas kernels: 0 us -> 24.4 us
  blocking collectives: 0 us -> 20.4 us
  starting transfers between devices: 4.91 us -> 25.3 us
  local copies, waits for them, and re-layouts: 17.6 us -> 2.48 us
  matrix products: 14.2 us -> 0 us
  between operations: 14.1 us -> 0.71 us
  other arithmetic: 5.92 us -> 0.17 us
    unnamed x2 -> x0, waiting for transfers between devices: 147 us -> none
    ppermute x0 -> x20, waiting for transfers between devices: none -> 52.8 us  [the longest x14 43.9 us: exchange(): got[d] = lax.ppermute(own[d], 'order', [(i, i ^ d) for i in range(NO)])]
    all_to_all x1 -> x0, waiting for transfers between devices: 49.4 us -> none  [body(): lax.all_to_all(spectrum, 'order', split_axis=1, concat_axis=2, tiled=True)]
    ppermute x0 -> x20, starting transfers between devices: none -> 25.3 us  [the longest x14 17.5 us: exchange(): got[d] = lax.ppermute(own[d], 'order', [(i, i ^ d) for i in range(NO)])]
    pallas_call x0 -> x4, Pallas kernels: none -> 24.4 us  [the longest x2 13.8 us: slots(): pl.pallas_call(functools.partial(slot_kernel, scale, start, aliased), gri...]
    all_to_all x0 -> x1, blocking collectives: none -> 20.4 us  [body(): lax.all_to_all(parts, 'dp', 0, 0, axis_index_groups=rings, tiled=True)]
    dot_general x6 -> x0, matrix products: 14.2 us -> none  [the longest x1 6.72 us: body(): jnp.einsum('ira,ac->cir', polar_grid, dft_table, preferred_element_type=j...]
    reshape x1 -> x0, local copies, waits for them, and re-layouts: 8.48 us -> none  [body(): spectrum = spectrum.reshape(2, slot_total, local_images, nodes)]
  transfers between devices with their start and end apart: 2 -> 20, of which waited for: 2 -> 11; matrix products, arithmetic and copies ran while one was open for 3% -> 0% of each run, Pallas kernels for 0% -> 8%
where the time goes in v1:
time: 127 us; the launch traced here: 126 us
  waiting for transfers between devices  52.8 us (42%)
  starting transfers between devices  25.3 us (20%)
  Pallas kernels  24.4 us (19%)
  blocking collectives  20.4 us (16%)
  local copies, waits for them, and re-layouts  2.48 us (2%)
    ppermute x14, waiting for transfers between devices, exchange(): got[d] = lax.ppermute(own[d], 'order', [(i, i ^ d) for i in range(NO)])  43.9 us
    all_to_all x1, blocking collectives, body(): lax.all_to_all(parts, 'dp', 0, 0, axis_index_groups=rings, tiled=True)  20.4 us
    ppermute x14, starting transfers between devices, exchange(): got[d] = lax.ppermute(own[d], 'order', [(i, i ^ d) for i in range(NO)])  17.5 us
    pallas_call x2, Pallas kernels, slots(): pl.pallas_call(functools.partial(slot_kernel, scale, start, aliased), gri...  13.8 us
    ppermute x6, waiting for transfers between devices, gather_y(): moved.append(lax.ppermute(covs[dy], 'dp', perm))  8.94 us
    pallas_call x1, Pallas kernels, spectra(): pl.pallas_call(spectrum_kernel, grid=(count // step,), in_specs=[pl.Block...  8.9 us
    ppermute x6, starting transfers between devices, gather_y(): moved.append(lax.ppermute(covs[dy], 'dp', perm))  7.78 us
  transfers between devices with their start and end apart: 20, of which 11 were waited for; matrix products, arithmetic and copies ran while one was open for 0% of the time, Pallas kernels for 8%

profile of v1, /device:TPU:24, one launch (start us, length us, event | category | flops | bytes accessed | tf_op | source)
XLA Modules:
  0.0 126.3 jit_solution(9163196412087918363)
XLA Ops:
  0.6 0.7 copy-done.3
  1.4 0.7 copy-done.4
  2.1 1.0 copy-done.5
  3.1 8.9 %spectra.1 = (bf16[32,48,128]{2,1,0:T(8,128)(2,1)S(1)}, bf16[32,48,128]{2,1,0:T(8,128)(2,1)S(1)}, bf16[32,48,128]{2,1,0:T(8,128)(2,1)S(1)}, bf16[32,48,128]{2,1,...) custom-call(bf16[32,128,512]{2,1,0:T(8,128)(2,1)} %x_ref.1, ...), custom_call_target="tpu_custom_call" | custom-call | flops 2684354560 | bytes 8388608 | tf_op jit(solution)/shard_map/spectra/pallas_call | solution.py:91
  12.0 0.1 collective-permute-start
  12.1 1.6 %collective-permute-start.1 = (bf16[32,48,128]{2,1,0:T(8,128)(2,1)S(1)}, bf16[32,48,128]{2,1,0:T(8,128)(2,1)S(1)}, u32[]{:S(2)}, u32[]{:S(2)}) collective-permute-start(bf16[32,48,128]{2,1,0:T(8,128)(2,1)S(1)} %get-tuple-element.30), channel_id=1, source_target_pairs={{0,2},{1,3},{2,0},{3,1},{4,6},{5,7},{6,4},{7,5},{8,10},{9,11},{10,... | collective-permute-start | bytes 1179656 | tf_op jit(solution)/shard_map/ppermute | solution.py:216
  13.7 0.1 collective-permute-start.10
  13.9 0.5 collective-permute-start.11
  14.4 1.2 collective-permute-start.2
  15.6 0.0 collective-permute-done.10.refs_1_
  15.6 2.7 %collective-permute-start.3 = (bf16[32,48,128]{2,1,0:T(8,128)(2,1)S(1)}, bf16[32,48,128]{2,1,0:T(8,128)(2,1)S(1)}, u32[]{:S(2)}, u32[]{:S(2)}) collective-permute-start(bf16[32,48,128]{2,1,0:T(8,128)(2,1)S(1)} %get-tuple-element.32), channel_id=1, source_target_pairs={{0,4},{1,5},{2,6},{3,7},{4,0},{5,1},{6,2},{7,3},{8,12},{9,13},{10,... | collective-permute-start | bytes 1179656 | tf_op jit(solution)/shard_map/ppermute | solution.py:216
  18.3 8.6 %collective-permute-done.11.refs_2_ = bf16[32,16,128]{2,1,0:T(8,128)(2,1)S(1)} collective-permute-done((bf16[32,16,128]{2,1,0:T(8,128)(2,1)S(1)}, bf16[32,16,128]{2,1,0:T(8,128)(2,1)S(1)}, u32[]{:S(2)}, u32[]{:S(2)}) %collective-permute-start.11) | collective-permute-done | bytes 131104 | tf_op jit(solution)/shard_map/ppermute | solution.py:216
  26.9 1.8 %collective-permute-start.4 = (bf16[32,48,128]{2,1,0:T(8,128)(2,1)S(1)}, bf16[32,48,128]{2,1,0:T(8,128)(2,1)S(1)}, u32[]{:S(2)}, u32[]{:S(2)}) collective-permute-start(bf16[32,48,128]{2,1,0:T(8,128)(2,1)S(1)} %get-tuple-element.33), channel_id=1, source_target_pairs={{0,5},{1,4},{2,7},{3,6},{4,1},{5,0},{6,3},{7,2},{8,13},{9,12},{10,... | collective-permute-start | bytes 1179656 | tf_op jit(solution)/shard_map/ppermute | solution.py:216
  28.7 0.0 collective-permute-done.refs_1_
  28.7 1.2 collective-permute-start.5
  29.9 0.0 collective-permute-done.1.refs_2_
  29.9 2.7 %collective-permute-start.6 = (bf16[32,48,128]{2,1,0:T(8,128)(2,1)S(1)}, bf16[32,48,128]{2,1,0:T(8,128)(2,1)S(1)}, u32[]{:S(2)}, u32[]{:S(2)}) collective-permute-start(bf16[32,48,128]{2,1,0:T(8,128)(2,1)S(1)} %get-tuple-element.35), channel_id=1, source_target_pairs={{0,7},{1,6},{2,5},{3,4},{4,3},{5,2},{6,1},{7,0},{8,15},{9,14},{10,... | collective-permute-start | bytes 1179656 | tf_op jit(solution)/shard_map/ppermute | solution.py:216
  32.6 1.8 %collective-permute-done.2.refs_3_ = bf16[32,48,128]{2,1,0:T(8,128)(2,1)S(1)} collective-permute-done((bf16[32,48,128]{2,1,0:T(8,128)(2,1)S(1)}, bf16[32,48,128]{2,1,0:T(8,128)(2,1)S(1)}, u32[]{:S(2)}, u32[]{:S(2)}) %collective-permute-start.2) | collective-permute-done | bytes 393248 | tf_op jit(solution)/shard_map/ppermute | solution.py:216
  34.4 2.2 %collective-permute-start.12 = (bf16[32,16,128]{2,1,0:T(8,128)(2,1)S(1)}, bf16[32,16,128]{2,1,0:T(8,128)(2,1)S(1)}, u32[]{:S(2)}, u32[]{:S(2)}) collective-permute-start(bf16[32,16,128]{2,1,0:T(8,128)(2,1)S(1)} %get-tuple-element.43), channel_id=1, source_target_pairs={{0,3},{1,2},{2,1},{3,0},{4,7},{5,6},{6,5},{7,4},{8,11},{9,10},{10,... | collective-permute-start | bytes 393224 | tf_op jit(solution)/shard_map/ppermute | solution.py:216
  36.6 9.5 %collective-permute-done.3.refs_4_ = bf16[32,48,128]{2,1,0:T(8,128)(2,1)S(1)} collective-permute-done((bf16[32,48,128]{2,1,0:T(8,128)(2,1)S(1)}, bf16[32,48,128]{2,1,0:T(8,128)(2,1)S(1)}, u32[]{:S(2)}, u32[]{:S(2)}) %collective-permute-start.3) | collective-permute-done | bytes 393248 | tf_op jit(solution)/shard_map/ppermute | solution.py:216
  46.1 0.8 collective-permute-start.13
  46.9 6.7 %collective-permute-done.4.refs_5_ = bf16[32,48,128]{2,1,0:T(8,128)(2,1)S(1)} collective-permute-done((bf16[32,48,128]{2,1,0:T(8,128)(2,1)S(1)}, bf16[32,48,128]{2,1,0:T(8,128)(2,1)S(1)}, u32[]{:S(2)}, u32[]{:S(2)}) %collective-permute-start.4) | collective-permute-done | bytes 393248 | tf_op jit(solution)/shard_map/ppermute | solution.py:216
  53.6 1.1 collective-permute-start.14
  54.7 9.4 %collective-permute-done.5.refs_6_ = bf16[32,48,128]{2,1,0:T(8,128)(2,1)S(1)} collective-permute-done((bf16[32,48,128]{2,1,0:T(8,128)(2,1)S(1)}, bf16[32,48,128]{2,1,0:T(8,128)(2,1)S(1)}, u32[]{:S(2)}, u32[]{:S(2)}) %collective-permute-start.5) | collective-permute-done | bytes 393248 | tf_op jit(solution)/shard_map/ppermute | solution.py:216
  64.1 1.2 collective-permute-start.15
  65.3 7.8 %collective-permute-done.6.refs_7_ = bf16[32,48,128]{2,1,0:T(8,128)(2,1)S(1)} collective-permute-done((bf16[32,48,128]{2,1,0:T(8,128)(2,1)S(1)}, bf16[32,48,128]{2,1,0:T(8,128)(2,1)S(1)}, u32[]{:S(2)}, u32[]{:S(2)}) %collective-permute-start.6) | collective-permute-done | bytes 393248 | tf_op jit(solution)/shard_map/ppermute | solution.py:216
  73.1 0.3 collective-permute-start.16
  73.4 9.7 %slots.2 = (bf16[2,4,8,256,128]{4,3,2,1,0:T(8,128)(2,1)}, bf16[6,128,128]{2,1,0:T(8,128)(2,1)S(1)}, bf16[6,128,128]{2,1,0:T(8,128)(2,1)S(1)}, bf16[6,128,128]{2,1,0:T(8,128)(2,1)S(1)}, bf16[6,128,128]{2,1,0:T(8,128)(2,1)S(1)}) custom-call(s32[32]{0:T(128)S(1)} %copy-done.2, bf16[32,48,128]{2,1,0:T(8,128)(2,1)S(1)} %get-tuple-element.28.refs_0_, ...), custom_call_target="tpu_custom_call" | custom-call | flops 805306368 | bytes 12582912 | tf_op jit(solution)/shard_map/slots/pallas_call | solution.py:171
  83.1 0.0 collective-permute-done.12.refs_3_
  83.1 0.0 collective-permute-done.13.refs_4_
  83.2 0.0 collective-permute-done.14.refs_5_
  83.2 0.0 collective-permute-done.15.refs_6_
  83.2 0.0 collective-permute-done.16.refs_7_
  83.2 4.1 %slots.3 = (bf16[2,4,8,256,128]{4,3,2,1,0:T(8,128)(2,1)}, bf16[2,128,128]{2,1,0:T(8,128)(2,1)S(1)}, bf16[2,128,128]{2,1,0:T(8,128)(2,1)S(1)}, bf16[2,128,128]{2,1,0:T(8,128)(2,1)S(1)}, bf16[2,128,128]{2,1,0:T(8,128)(2,1)S(1)}) custom-call(s32[32]{0:T(128)S(1)} %copy-done.2, ...), custom_call_target="tpu_custom_call", output_to_operand_aliasing={{0}: (11, {})} | custom-call | flops 268435456 | bytes 4194304 | tf_op jit(solution)/shard_map/slots/pallas_call | solution.py:171
  87.3 1.2 collective-permute-start.17
  88.5 0.8 collective-permute-start.18
  89.3 2.1 %collective-permute-start.19 = (bf16[2,128,128]{2,1,0:T(8,128)(2,1)S(1)}, bf16[2,128,128]{2,1,0:T(8,128)(2,1)S(1)}, u32[]{:S(2)}, u32[]{:S(2)}) collective-permute-start(bf16[2,128,128]{2,1,0:T(8,128)(2,1)S(1)} %get-tuple-element.52), channel_id=1, source_target_pairs={{0,192},{8,200},{16,208},{24,216},{32,224},{40,232},{48,240},{56,2... | collective-permute-start | bytes 196616 | tf_op jit(solution)/shard_map/ppermute | solution.py:223
  91.4 1.2 collective-permute-start.7
  92.6 0.8 collective-permute-start.8
  93.4 0.4 collective-permute-done.17
  93.8 1.6 %collective-permute-start.9 = (bf16[6,128,128]{2,1,0:T(8,128)(2,1)S(1)}, bf16[6,128,128]{2,1,0:T(8,128)(2,1)S(1)}, u32[]{:S(2)}, u32[]{:S(2)}) collective-permute-start(bf16[6,128,128]{2,1,0:T(8,128)(2,1)S(1)} %get-tuple-element.39), channel_id=1, source_target_pairs={{0,192},{8,200},{16,208},{24,216},{32,224},{40,232},{48,240},{56,2... | collective-permute-start | bytes 589832 | tf_op jit(solution)/shard_map/ppermute | solution.py:223
  95.5 1.8 %collective-permute-done.19 = bf16[2,128,128]{2,1,0:T(8,128)(2,1)S(1)} collective-permute-done((bf16[2,128,128]{2,1,0:T(8,128)(2,1)S(1)}, bf16[2,128,128]{2,1,0:T(8,128)(2,1)S(1)}, u32[]{:S(2)}, u32[]{:S(2)}) %collective-permute-start.19) | collective-permute-done | bytes 65568 | tf_op jit(solution)/shard_map/ppermute | solution.py:223
  97.4 3.3 %collective-permute-done.7 = bf16[6,128,128]{2,1,0:T(8,128)(2,1)S(1)} collective-permute-done((bf16[6,128,128]{2,1,0:T(8,128)(2,1)S(1)}, bf16[6,128,128]{2,1,0:T(8,128)(2,1)S(1)}, u32[]{:S(2)}, u32[]{:S(2)}) %collective-permute-start.7) | collective-permute-done | bytes 196640 | tf_op jit(solution)/shard_map/ppermute | solution.py:223
  100.6 1.4 %collective-permute-done.8 = bf16[6,128,128]{2,1,0:T(8,128)(2,1)S(1)} collective-permute-done((bf16[6,128,128]{2,1,0:T(8,128)(2,1)S(1)}, bf16[6,128,128]{2,1,0:T(8,128)(2,1)S(1)}, u32[]{:S(2)}, u32[]{:S(2)}) %collective-permute-start.8) | collective-permute-done | bytes 196640 | tf_op jit(solution)/shard_map/ppermute | solution.py:223
  102.0 2.0 %collective-permute-done.9 = bf16[6,128,128]{2,1,0:T(8,128)(2,1)S(1)} collective-permute-done((bf16[6,128,128]{2,1,0:T(8,128)(2,1)S(1)}, bf16[6,128,128]{2,1,0:T(8,128)(2,1)S(1)}, u32[]{:S(2)}, u32[]{:S(2)}) %collective-permute-start.9) | collective-permute-done | bytes 196640 | tf_op jit(solution)/shard_map/ppermute | solution.py:223
  104.0 0.1 add_convert_fusion
  104.2 20.4 %all_to_all.5.parts_ref = bf16[8,128,128]{2,1,0:T(8,128)(2,1)} all-to-all(bf16[8,128,128]{2,1,0:T(8,128)(2,1)S(1)} %pad_maximum_fusion), channel_id=1, replica_groups={{0,8,16,24,32,40,48,56},{64,72,80,88,96,104,112,120},{128,136,144,152,1..., dimensions={0} | all-to-all | bytes 524288 | tf_op jit(solution)/shard_map/all_to_all | solution.py:239
  124.6 1.7 %finish.1 = f32[2,128,128]{2,1,0:T(8,128)} custom-call(bf16[8,128,128]{2,1,0:T(8,128)(2,1)} %all_to_all.5.parts_ref), custom_call_target="tpu_custom_call" | custom-call | tf_op jit(solution)/shard_map/finish/pallas_call | solution.py:240
  (12 shorter events, 0.1 us)
Async XLA Ops:
  0.6 0.8 copy-start.3
  1.4 0.7 copy-start.4
  2.1 1.0 copy-start.5
  3.1 70.3 %copy-start = (bf16[32,128,128]{2,1,0:T(8,128)(2,1)S(1)}, bf16[32,128,128]{2,1,0:T(8,128)(2,1)}, u32[]{:S(2)}) copy-start(bf16[32,128,128]{2,1,0:T(8,128)(2,1)} %param.11) | copy-start | bytes 3145732
  3.1 70.3 %copy-start.1 = (bf16[32,128,128]{2,1,0:T(8,128)(2,1)S(1)}, bf16[32,128,128]{2,1,0:T(8,128)(2,1)}, u32[]{:S(2)}) copy-start(bf16[32,128,128]{2,1,0:T(8,128)(2,1)} %param.12) | copy-start | bytes 3145732
  3.1 70.3 %copy-start.2 = (s32[32]{0:T(128)S(1)}, s32[32]{0:T(128)}, u32[]{:S(2)}) copy-start(s32[32]{0:T(128)} %counts_ref.3) | copy-start | bytes 388
  12.0 16.7 %collective-permute-start = (bf16[32,48,128]{2,1,0:T(8,128)(2,1)S(1)}, bf16[32,48,128]{2,1,0:T(8,128)(2,1)S(1)}, u32[]{:S(2)}, u32[]{:S(2)}) collective-permute-start(bf16[32,48,128]{2,1,0:T(8,128)(2,1)S(1)} %get-tuple-element.29), channel_id=1, source_target_pairs={{0,1},{1,0},{2,3},{3,2},{4,5},{5,4},{6,7},{7,6},{8,9},{9,8},{10,11... | collective-permute-start | bytes 1179656 | tf_op jit(solution)/shard_map/ppermute | solution.py:216
  12.1 17.8 %collective-permute-start.1 = (bf16[32,48,128]{2,1,0:T(8,128)(2,1)S(1)}, bf16[32,48,128]{2,1,0:T(8,128)(2,1)S(1)}, u32[]{:S(2)}, u32[]{:S(2)}) collective-permute-start(bf16[32,48,128]{2,1,0:T(8,128)(2,1)S(1)} %get-tuple-element.30), channel_id=1, source_target_pairs={{0,2},{1,3},{2,0},{3,1},{4,6},{5,7},{6,4},{7,5},{8,10},{9,11},{10,... | collective-permute-start | bytes 1179656 | tf_op jit(solution)/shard_map/ppermute | solution.py:216
  13.7 1.9 %collective-permute-start.10 = (bf16[32,16,128]{2,1,0:T(8,128)(2,1)S(1)}, bf16[32,16,128]{2,1,0:T(8,128)(2,1)S(1)}, u32[]{:S(2)}, u32[]{:S(2)}) collective-permute-start(bf16[32,16,128]{2,1,0:T(8,128)(2,1)S(1)} %get-tuple-element.41), channel_id=1, source_target_pairs={{0,1},{1,0},{2,3},{3,2},{4,5},{5,4},{6,7},{7,6},{8,9},{9,8},{10,11... | collective-permute-start | bytes 393224 | tf_op jit(solution)/shard_map/ppermute | solution.py:216
  13.9 13.1 %collective-permute-start.11 = (bf16[32,16,128]{2,1,0:T(8,128)(2,1)S(1)}, bf16[32,16,128]{2,1,0:T(8,128)(2,1)S(1)}, u32[]{:S(2)}, u32[]{:S(2)}) collective-permute-start(bf16[32,16,128]{2,1,0:T(8,128)(2,1)S(1)} %get-tuple-element.42), channel_id=1, source_target_pairs={{0,2},{1,3},{2,0},{3,1},{4,6},{5,7},{6,4},{7,5},{8,10},{9,11},{10,... | collective-permute-start | bytes 393224 | tf_op jit(solution)/shard_map/ppermute | solution.py:216
  14.4 20.0 %collective-permute-start.2 = (bf16[32,48,128]{2,1,0:T(8,128)(2,1)S(1)}, bf16[32,48,128]{2,1,0:T(8,128)(2,1)S(1)}, u32[]{:S(2)}, u32[]{:S(2)}) collective-permute-start(bf16[32,48,128]{2,1,0:T(8,128)(2,1)S(1)} %get-tuple-element.31), channel_id=1, source_target_pairs={{0,3},{1,2},{2,1},{3,0},{4,7},{5,6},{6,5},{7,4},{8,11},{9,10},{10,... | collective-permute-start | bytes 1179656 | tf_op jit(solution)/shard_map/ppermute | solution.py:216
  15.6 30.5 %collective-permute-start.3 = (bf16[32,48,128]{2,1,0:T(8,128)(2,1)S(1)}, bf16[32,48,128]{2,1,0:T(8,128)(2,1)S(1)}, u32[]{:S(2)}, u32[]{:S(2)}) collective-permute-start(bf16[32,48,128]{2,1,0:T(8,128)(2,1)S(1)} %get-tuple-element.32), channel_id=1, source_target_pairs={{0,4},{1,5},{2,6},{3,7},{4,0},{5,1},{6,2},{7,3},{8,12},{9,13},{10,... | collective-permute-start | bytes 1179656 | tf_op jit(solution)/shard_map/ppermute | solution.py:216
  26.9 26.6 %collective-permute-start.4 = (bf16[32,48,128]{2,1,0:T(8,128)(2,1)S(1)}, bf16[32,48,128]{2,1,0:T(8,128)(2,1)S(1)}, u32[]{:S(2)}, u32[]{:S(2)}) collective-permute-start(bf16[32,48,128]{2,1,0:T(8,128)(2,1)S(1)} %get-tuple-element.33), channel_id=1, source_target_pairs={{0,5},{1,4},{2,7},{3,6},{4,1},{5,0},{6,3},{7,2},{8,13},{9,12},{10,... | collective-permute-start | bytes 1179656 | tf_op jit(solution)/shard_map/ppermute | solution.py:216
  28.7 35.4 %collective-permute-start.5 = (bf16[32,48,128]{2,1,0:T(8,128)(2,1)S(1)}, bf16[32,48,128]{2,1,0:T(8,128)(2,1)S(1)}, u32[]{:S(2)}, u32[]{:S(2)}) collective-permute-start(bf16[32,48,128]{2,1,0:T(8,128)(2,1)S(1)} %get-tuple-element.34), channel_id=1, source_target_pairs={{0,6},{1,7},{2,4},{3,5},{4,2},{5,3},{6,0},{7,1},{8,14},{9,15},{10,... | collective-permute-start | bytes 1179656 | tf_op jit(solution)/shard_map/ppermute | solution.py:216
  29.9 43.2 %collective-permute-start.6 = (bf16[32,48,128]{2,1,0:T(8,128)(2,1)S(1)}, bf16[32,48,128]{2,1,0:T(8,128)(2,1)S(1)}, u32[]{:S(2)}, u32[]{:S(2)}) collective-permute-start(bf16[32,48,128]{2,1,0:T(8,128)(2,1)S(1)} %get-tuple-element.35), channel_id=1, source_target_pairs={{0,7},{1,6},{2,5},{3,4},{4,3},{5,2},{6,1},{7,0},{8,15},{9,14},{10,... | collective-permute-start | bytes 1179656 | tf_op jit(solution)/shard_map/ppermute | solution.py:216
  34.4 48.7 %collective-permute-start.12 = (bf16[32,16,128]{2,1,0:T(8,128)(2,1)S(1)}, bf16[32,16,128]{2,1,0:T(8,128)(2,1)S(1)}, u32[]{:S(2)}, u32[]{:S(2)}) collective-permute-start(bf16[32,16,128]{2,1,0:T(8,128)(2,1)S(1)} %get-tuple-element.43), channel_id=1, source_target_pairs={{0,3},{1,2},{2,1},{3,0},{4,7},{5,6},{6,5},{7,4},{8,11},{9,10},{10,... | collective-permute-start | bytes 393224 | tf_op jit(solution)/shard_map/ppermute | solution.py:216
  46.1 37.1 %collective-permute-start.13 = (bf16[32,16,128]{2,1,0:T(8,128)(2,1)S(1)}, bf16[32,16,128]{2,1,0:T(8,128)(2,1)S(1)}, u32[]{:S(2)}, u32[]{:S(2)}) collective-permute-start(bf16[32,16,128]{2,1,0:T(8,128)(2,1)S(1)} %get-tuple-element.44), channel_id=1, source_target_pairs={{0,4},{1,5},{2,6},{3,7},{4,0},{5,1},{6,2},{7,3},{8,12},{9,13},{10,... | collective-permute-start | bytes 393224 | tf_op jit(solution)/shard_map/ppermute | solution.py:216
  53.6 29.6 %collective-permute-start.14 = (bf16[32,16,128]{2,1,0:T(8,128)(2,1)S(1)}, bf16[32,16,128]{2,1,0:T(8,128)(2,1)S(1)}, u32[]{:S(2)}, u32[]{:S(2)}) collective-permute-start(bf16[32,16,128]{2,1,0:T(8,128)(2,1)S(1)} %get-tuple-element.45), channel_id=1, source_target_pairs={{0,5},{1,4},{2,7},{3,6},{4,1},{5,0},{6,3},{7,2},{8,13},{9,12},{10,... | collective-permute-start | bytes 393224 | tf_op jit(solution)/shard_map/ppermute | solution.py:216
  64.1 19.1 %collective-permute-start.15 = (bf16[32,16,128]{2,1,0:T(8,128)(2,1)S(1)}, bf16[32,16,128]{2,1,0:T(8,128)(2,1)S(1)}, u32[]{:S(2)}, u32[]{:S(2)}) collective-permute-start(bf16[32,16,128]{2,1,0:T(8,128)(2,1)S(1)} %get-tuple-element.46), channel_id=1, source_target_pairs={{0,6},{1,7},{2,4},{3,5},{4,2},{5,3},{6,0},{7,1},{8,14},{9,15},{10,... | collective-permute-start | bytes 393224 | tf_op jit(solution)/shard_map/ppermute | solution.py:216
  73.1 10.1 %collective-permute-start.16 = (bf16[32,16,128]{2,1,0:T(8,128)(2,1)S(1)}, bf16[32,16,128]{2,1,0:T(8,128)(2,1)S(1)}, u32[]{:S(2)}, u32[]{:S(2)}) collective-permute-start(bf16[32,16,128]{2,1,0:T(8,128)(2,1)S(1)} %get-tuple-element.47), channel_id=1, source_target_pairs={{0,7},{1,6},{2,5},{3,4},{4,3},{5,2},{6,1},{7,0},{8,15},{9,14},{10,... | collective-permute-start | bytes 393224 | tf_op jit(solution)/shard_map/ppermute | solution.py:216
  87.3 6.5 %collective-permute-start.17 = (bf16[2,128,128]{2,1,0:T(8,128)(2,1)S(1)}, bf16[2,128,128]{2,1,0:T(8,128)(2,1)S(1)}, u32[]{:S(2)}, u32[]{:S(2)}) collective-permute-start(bf16[2,128,128]{2,1,0:T(8,128)(2,1)S(1)} %get-tuple-element.50), channel_id=1, source_target_pairs={{0,128},{8,136},{16,144},{24,152},{32,160},{40,168},{48,176},{56,1... | collective-permute-start | bytes 196616 | tf_op jit(solution)/shard_map/ppermute | solution.py:223
  88.5 7.0 %collective-permute-start.18 = (bf16[2,128,128]{2,1,0:T(8,128)(2,1)S(1)}, bf16[2,128,128]{2,1,0:T(8,128)(2,1)S(1)}, u32[]{:S(2)}, u32[]{:S(2)}) collective-permute-start(bf16[2,128,128]{2,1,0:T(8,128)(2,1)S(1)} %get-tuple-element.51), channel_id=1, source_target_pairs={{0,64},{8,72},{16,80},{24,88},{32,96},{40,104},{48,112},{56,120},{... | collective-permute-start | bytes 196616 | tf_op jit(solution)/shard_map/ppermute | solution.py:223
  89.3 8.0 %collective-permute-start.19 = (bf16[2,128,128]{2,1,0:T(8,128)(2,1)S(1)}, bf16[2,128,128]{2,1,0:T(8,128)(2,1)S(1)}, u32[]{:S(2)}, u32[]{:S(2)}) collective-permute-start(bf16[2,128,128]{2,1,0:T(8,128)(2,1)S(1)} %get-tuple-element.52), channel_id=1, source_target_pairs={{0,192},{8,200},{16,208},{24,216},{32,224},{40,232},{48,240},{56,2... | collective-permute-start | bytes 196616 | tf_op jit(solution)/shard_map/ppermute | solution.py:223
  91.4 9.2 %collective-permute-start.7 = (bf16[6,128,128]{2,1,0:T(8,128)(2,1)S(1)}, bf16[6,128,128]{2,1,0:T(8,128)(2,1)S(1)}, u32[]{:S(2)}, u32[]{:S(2)}) collective-permute-start(bf16[6,128,128]{2,1,0:T(8,128)(2,1)S(1)} %get-tuple-element.37), channel_id=1, source_target_pairs={{0,128},{8,136},{16,144},{24,152},{32,160},{40,168},{48,176},{56,1... | collective-permute-start | bytes 589832 | tf_op jit(solution)/shard_map/ppermute | solution.py:223
  92.6 9.5 %collective-permute-start.8 = (bf16[6,128,128]{2,1,0:T(8,128)(2,1)S(1)}, bf16[6,128,128]{2,1,0:T(8,128)(2,1)S(1)}, u32[]{:S(2)}, u32[]{:S(2)}) collective-permute-start(bf16[6,128,128]{2,1,0:T(8,128)(2,1)S(1)} %get-tuple-element.38), channel_id=1, source_target_pairs={{0,64},{8,72},{16,80},{24,88},{32,96},{40,104},{48,112},{56,120},{... | collective-permute-start | bytes 589832 | tf_op jit(solution)/shard_map/ppermute | solution.py:223
  93.8 10.2 %collective-permute-start.9 = (bf16[6,128,128]{2,1,0:T(8,128)(2,1)S(1)}, bf16[6,128,128]{2,1,0:T(8,128)(2,1)S(1)}, u32[]{:S(2)}, u32[]{:S(2)}) collective-permute-start(bf16[6,128,128]{2,1,0:T(8,128)(2,1)S(1)} %get-tuple-element.39), channel_id=1, source_target_pairs={{0,192},{8,200},{16,208},{24,216},{32,224},{40,232},{48,240},{56,2... | collective-permute-start | bytes 589832 | tf_op jit(solution)/shard_map/ppermute | solution.py:223

commit v2 on v1

v2 whole, which is shorter than its diff:
```python
import functools
import math

import numpy as np
import jax
import jax.numpy as jnp
from jax import lax
from jax.experimental import pallas as pl
from jax.experimental.pallas import tpu as pltpu
from jax.sharding import PartitionSpec as P

NY, NZ = 4, 8
NO = 8
GROUPS = 4
FIRST = 3
SPLIT = (4, 5)
WHOLE = (2, 6, 3, 7, 1, 0)
HEIGHT = 16
STARTS = [GROUPS * HEIGHT * d for d in SPLIT + WHOLE]
STARTS += [GROUPS * HEIGHT * d + FIRST * HEIGHT for d in SPLIT]
HEIGHTS = [FIRST * HEIGHT] * len(SPLIT) + [GROUPS * HEIGHT] * len(WHOLE)
HEIGHTS += [(GROUPS - FIRST) * HEIGHT] * len(SPLIT)


def angle_tables(samples, orders):
    product = np.arange(orders)[:, None] * np.arange(samples)[None, :] % samples
    theta = product * (2.0 * math.pi / samples)
    factor = 1.0 / math.sqrt(samples)
    both = np.stack([np.cos(theta), -np.sin(theta)]) * factor
    return both.astype(np.float32).astype(jnp.bfloat16)


def spectrum_kernel(x_ref, interp_ref, slots_ref, tables_ref, *rest):
    outs, table = rest[:-1], rest[-1]
    total = tables_ref.shape[1]
    samples = tables_ref.shape[2]

    @pl.when(pl.program_id(0) == 0)
    def _():
        me = lax.axis_index("order")
        y = lax.axis_index("dp") // NZ
        s = lax.broadcasted_iota(jnp.int32, (total, total), 0)
        d, g, dy, zl = s >> 5, (s >> 3) & 3, (s >> 1) & 3, s & 1
        slot = (me ^ d) * (NY * NZ) + (y ^ dy) * NZ + g * 2 + zl
        lane = lax.broadcasted_iota(jnp.int32, (total, total), 1)
        pick = (slot == lane).astype(jnp.bfloat16)
        holds = (slots_ref[...] == s).astype(jnp.bfloat16)
        hot = lax.dot_general(
            pick, holds, (((1,), (1,)), ((), ())), preferred_element_type=jnp.float32
        ).astype(jnp.bfloat16)
        both = [
            jnp.dot(hot, tables_ref[p], preferred_element_type=jnp.float32).reshape(
                total // 8, 1, 8, samples
            )
            for p in range(2)
        ]
        table[...] = (
            jnp.concatenate(both, axis=1).reshape(2 * total, samples).astype(jnp.bfloat16)
        )

    n, radii = x_ref.shape[0], x_ref.shape[1]
    interp = interp_ref[...]
    nodes = interp.shape[1]
    zero = jnp.zeros_like(interp)
    both = jnp.concatenate(
        [jnp.concatenate([interp, zero], axis=1), jnp.concatenate([zero, interp], axis=1)], axis=0
    )
    first = pl.program_id(0) * n
    for i in range(0, n, 2):
        polar = lax.dot_general(
            x_ref[i : i + 2].reshape(2 * radii, samples), both, (((0,), (0,)), ((), ())),
            preferred_element_type=jnp.float32,
        ).astype(jnp.bfloat16)
        spec = jnp.dot(table[...], polar, preferred_element_type=jnp.float32).astype(jnp.bfloat16)
        for out, base in zip(outs, STARTS):
            rows = out.shape[1]
            for h in range(2):
                out[first + i + h] = spec[base : base + rows, h * nodes : (h + 1) * nodes]


def in_hbm(x):
    return pltpu.with_memory_space_constraint(x, pltpu.HBM)


def spectra(images, interp, assignment):
    count, radii, samples = images.shape
    nodes = interp.shape[1]
    total = assignment.shape[0]
    step = 8
    tables = jnp.asarray(angle_tables(samples, total))
    return pl.pallas_call(
        spectrum_kernel,
        grid=(count // step,),
        in_specs=[
            pl.BlockSpec((step, radii, samples), lambda i: (i, 0, 0)),
            pl.BlockSpec((radii, nodes), lambda i: (0, 0)),
            pl.BlockSpec((1, total), lambda i: (0, 0)),
            pl.BlockSpec((2, total, samples), lambda i: (0, 0, 0)),
        ],
        out_specs=[pl.BlockSpec(memory_space=pltpu.VMEM)] * len(HEIGHTS),
        out_shape=[jax.ShapeDtypeStruct((count, h, nodes), jnp.bfloat16) for h in HEIGHTS],
        scratch_shapes=[pltpu.VMEM((2 * total, samples), jnp.bfloat16)],
        compiler_params=pltpu.CompilerParams(vmem_limit_bytes=40 << 20),
        cost_estimate=pl.CostEstimate(
            flops=2 * count * nodes * samples * (radii + 2 * total),
            bytes_accessed=4 * count * radii * samples,
            transcendentals=0,
        ),
        name="spectra",
    )(*(in_hbm(x) for x in (images, interp, assignment[None, :], tables)))


def slot_kernel(scale, start, counts_ref, *refs):
    pieces, basis_ref = refs[:NO], refs[NO]
    coef_ref, covs, turned = refs[NO + 1], refs[NO + 2 : NO + 2 + NY], refs[-1]
    me = lax.axis_index("order")
    y = lax.axis_index("dp") // NZ
    group = start + pl.program_id(0)
    images, rows, nodes = pieces[0].shape
    for i, d in enumerate(SPLIT + WHOLE):
        turned[d] = jnp.swapaxes(pieces[i][...], 0, 1)
    width = basis_ref.shape[3]
    lane = lax.broadcasted_iota(jnp.int32, (nodes, width), 1)
    row = lax.broadcasted_iota(jnp.int32, (width, width), 0)
    col = lax.broadcasted_iota(jnp.int32, (width, width), 1)
    upper = row <= col
    for dy in range(NY):
        yy = y ^ dy
        for zl in range(2):
            limit = counts_ref[yy * NZ + group * 2 + zl]
            basis = jnp.where(lane < limit, basis_ref[yy, zl], 0)
            spec = jnp.concatenate(
                [
                    turned[me ^ j, p * 8 + dy * 2 + zl]
                    for p in range(2)
                    for j in range(NO)
                ],
                axis=0,
            )
            coef = jnp.dot(spec, basis, preferred_element_type=jnp.float32).astype(jnp.bfloat16)
            half = coef.shape[0] // 2
            coef_ref[0, yy, zl] = coef[:half]
            coef_ref[1, yy, zl] = coef[half:]
            pair = jnp.concatenate([coef[:half], coef[half:]], axis=1)
            gram = lax.dot_general(
                pair, pair, (((0,), (0,)), ((), ())), preferred_element_type=jnp.float32
            )
            real = gram[:width, :width] + gram[width:, width:]
            imag = gram[width:, :width] - gram[:width, width:]
            covs[dy][zl] = (jnp.where(upper, real, imag) * scale).astype(jnp.bfloat16)


def slots(pieces, counts, basis, scale, start, groups):
    images, _, nodes = pieces[0].shape
    _, _, _, width = basis.shape
    rows = HEIGHT
    total = NO * images
    part = pl.BlockSpec((images, rows, nodes), lambda g, c: (0, g, 0))
    whole = pl.BlockSpec((images, rows, nodes), lambda g, c: (0, start + g, 0))
    weights = pl.BlockSpec((NY, 2, nodes, width), lambda g, c: (0, start + g, 0, 0))
    return pl.pallas_call(
        functools.partial(slot_kernel, scale, start),
        grid_spec=pltpu.PrefetchScalarGridSpec(
            num_scalar_prefetch=1,
            grid=(groups,),
            in_specs=[part] * len(SPLIT) + [whole] * len(WHOLE) + [weights],
            out_specs=[pl.BlockSpec((2, NY, 2, total, width), lambda g, c: (0, 0, g, 0, 0))]
            + [pl.BlockSpec((2, width, width), lambda g, c: (g, 0, 0))] * NY,
            scratch_shapes=[pltpu.VMEM((NO, rows, images, nodes), jnp.bfloat16)],
        ),
        out_shape=[pltpu.HBM((2, NY, 2 * groups, total, width), jnp.bfloat16)]
        + [jax.ShapeDtypeStruct((2 * groups, width, width), jnp.bfloat16)] * NY,
        compiler_params=pltpu.CompilerParams(vmem_limit_bytes=32 << 20),
        cost_estimate=pl.CostEstimate(
            flops=groups * 64 * 6 * total * nodes * width,
            bytes_accessed=groups * 3 << 20,
            transcendentals=0,
        ),
        name="slots",
    )(counts, *pieces, basis)


def project_kernel(first_ref, second_ref, eigen_ref, out_ref):
    groups = first_ref.shape[2] // 2

    def run(coef_ref):
        for y in range(NY):
            for zl in range(2):
                for p in range(2):
                    out_ref[p, y, zl] = jnp.dot(
                        coef_ref[p, y, zl], eigen_ref[y, zl], preferred_element_type=jnp.float32
                    ).astype(jnp.bfloat16)

    late = pl.program_id(0) >= FIRST

    @pl.when(jnp.logical_not(late))
    def _():
        run(first_ref)

    @pl.when(late)
    def _():
        run(second_ref)


def project(first, second, eigen):
    _, _, _, total, width = first.shape
    ends = eigen.shape[3]
    held = (2, NY, 2, total, width)
    return pl.pallas_call(
        project_kernel,
        grid=(GROUPS,),
        in_specs=[
            pl.BlockSpec(held, lambda g: (0, 0, jnp.minimum(g, FIRST - 1), 0, 0)),
            pl.BlockSpec(held, lambda g: (0, 0, jnp.maximum(g - FIRST, 0), 0, 0)),
            pl.BlockSpec((NY, 2, width, ends), lambda g: (0, g, 0, 0)),
        ],
        out_specs=pl.BlockSpec((2, NY, 2, total, ends), lambda g: (0, 0, g, 0, 0)),
        out_shape=jax.ShapeDtypeStruct((2, NY, NZ, total, ends), jnp.bfloat16),
        compiler_params=pltpu.CompilerParams(vmem_limit_bytes=32 << 20),
        cost_estimate=pl.CostEstimate(
            flops=4 * NY * NZ * total * width * ends, bytes_accessed=9 << 20, transcendentals=0
        ),
        name="project",
    )(in_hbm(first), in_hbm(second), in_hbm(eigen))


def join_kernel(*refs):
    ins, out_ref = refs[:-1], refs[-1]
    done = 0
    for part in (ins[:NY], ins[NY:]):
        held = part[0].shape[0]
        added = part[0][...].astype(jnp.float32)
        for moved in part[1:]:
            added += moved[...].astype(jnp.float32)
        out_ref[done : done + held] = added.astype(jnp.bfloat16)
        done += held


def finish_kernel(parts_ref, out_ref):
    packed = parts_ref[0].astype(jnp.float32)
    for i in range(1, parts_ref.shape[0]):
        packed += parts_ref[i].astype(jnp.float32)
    other = packed.T
    row = lax.broadcasted_iota(jnp.int32, packed.shape, 0)
    col = lax.broadcasted_iota(jnp.int32, packed.shape, 1)
    out_ref[0] = jnp.where(row <= col, packed, other)
    out_ref[1] = jnp.where(row > col, packed, jnp.where(row < col, -other, 0.0))


def body(images, radial_interp, assignment, counts, radial_basis, eigenbasis):
    owned = radial_basis.shape[0]
    width = radial_basis.shape[2]
    total = images.shape[0] * lax.axis_size("order") * lax.axis_size("dp")
    pieces = spectra(images, radial_interp, assignment)

    basis = radial_basis.reshape(NY, NZ, radial_basis.shape[1], width)
    eigen = eigenbasis.reshape(NY, NZ, width, eigenbasis.shape[2])

    def exchange(own, partners):
        return [
            lax.ppermute(piece, "order", [(i, i ^ d) for i in range(NO)])
            for piece, d in zip(own, partners)
        ]

    def to_y(covs):
        return [
            lax.ppermute(covs[dy], "dp", [(i, i ^ (dy * NZ)) for i in range(NY * NZ)])
            for dy in range(1, NY)
        ]

    scale = 1.0 / total
    far, near = len(SPLIT), len(SPLIT) + len(WHOLE)
    first = exchange(pieces[:far], SPLIT)
    whole = exchange(pieces[far : near - 1], WHOLE) + [pieces[near - 1]]
    *gated, first[0], first[1] = lax.optimization_barrier(tuple(pieces[near:]) + tuple(first))
    second = exchange(gated, SPLIT) + whole
    first += whole
    coef_first, *cov_first = slots(first, counts, basis, scale, 0, FIRST)
    moved_first = to_y(cov_first)
    coef_second, *cov_second = slots(second, counts, basis, scale, FIRST, GROUPS - FIRST)
    moved_second = to_y(cov_second)
    projected = project(coef_first, coef_second, eigen)
    parts = pl.pallas_call(
        join_kernel,
        out_shape=jax.ShapeDtypeStruct((NZ, width, width), jnp.bfloat16),
        compiler_params=pltpu.CompilerParams(vmem_limit_bytes=8 << 20),
        name="join",
    )(cov_first[0], *moved_first, cov_second[0], *moved_second)
    rings = [[y * NZ + z for z in range(NZ)] for y in range(NY)]
    parts = lax.all_to_all(parts, "dp", 0, 0, axis_index_groups=rings, tiled=True)
    covariance = pl.pallas_call(
        finish_kernel,
        out_shape=jax.ShapeDtypeStruct((2, width, width), jnp.float32),
        compiler_params=pltpu.CompilerParams(vmem_limit_bytes=8 << 20),
        name="finish",
    )(parts)
    projected = projected.reshape(2, owned, projected.shape[3], projected.shape[4])
    return (covariance.reshape(1, 2 * width * width), projected)


def solution(mesh):
    placed = (
        P(("dp", "order"), None, None),
        P(),
        P(),
        P("order"),
        P("order", None, None),
        P("order", None, None),
    )
    return jax.shard_map(
        body,
        mesh=mesh,
        in_specs=placed,
        out_specs=(P(("order", "dp"), None), P(None, "order", "dp", None)),
        check_vma=False,
    )
```

time: 127 us -> 98.2 us (0.77)
  blocking collectives: 20.4 us -> 0 us
  waiting for transfers between devices: 52.8 us -> 45.8 us
  starting transfers between devices: 25.3 us -> 27.9 us
  local copies, waits for them, and re-layouts: 2.48 us -> 0.01 us
  Pallas kernels: 24.4 us -> 22.5 us
    all_to_all x1 -> x0, blocking collectives: 20.4 us -> none  [body(): lax.all_to_all(parts, 'dp', 0, 0, axis_index_groups=rings, tiled=True)]
    ppermute x20 -> x15, waiting for transfers between devices: 52.8 us -> 41.3 us  [the longest x9 34.5 us: exchange(): lax.ppermute(piece, 'order', [(i, i ^ d) for i in range(NO)])]
    all_to_all x0 -> x1, starting transfers between devices: none -> 8.47 us  [body(): lax.all_to_all(parts, 'dp', 0, 0, axis_index_groups=rings, tiled=True)]
    ppermute x20 -> x15, starting transfers between devices: 25.3 us -> 19.4 us  [the longest x9 9.87 us: exchange(): lax.ppermute(piece, 'order', [(i, i ^ d) for i in range(NO)])]
    all_to_all x0 -> x1, waiting for transfers between devices: none -> 4.55 us  [body(): lax.all_to_all(parts, 'dp', 0, 0, axis_index_groups=rings, tiled=True)]
    unnamed x12 -> x4, local copies, waits for them, and re-layouts: 2.48 us -> 0.01 us
    pallas_call x1, Pallas kernels: 8.9 us -> 6.82 us  [spectra(): pl.pallas_call(spectrum_kernel, grid=(count // step,), in_specs=[pl.Block...]
    pallas_call x2 -> x4, Pallas kernels: 13.8 us -> 14.9 us  [the longest x2 8.14 us: slots(): pl.pallas_call(functools.partial(slot_kernel, scale, start), grid_spec=pl...]
  transfers between devices with their start and end apart: 20 -> 16, of which waited for: 11 -> 9; matrix products, arithmetic and copies ran while one was open for 0% -> 0% of each run, Pallas kernels for 8% -> 15%
where the time goes in v2:
time: 98.2 us; the launch traced here: 96.9 us
  waiting for transfers between devices  45.8 us (47%)
  starting transfers between devices  27.9 us (28%)
  Pallas kernels  22.5 us (23%)
    ppermute x9, waiting for transfers between devices, exchange(): lax.ppermute(piece, 'order', [(i, i ^ d) for i in range(NO)])  34.5 us
    ppermute x9, starting transfers between devices, exchange(): lax.ppermute(piece, 'order', [(i, i ^ d) for i in range(NO)])  9.87 us
    ppermute x6, starting transfers between devices, to_y(): lax.ppermute(covs[dy], 'dp', [(i, i ^ dy * NZ) for i in range(NY * NZ)])  9.56 us
    all_to_all x1, starting transfers between devices, body(): lax.all_to_all(parts, 'dp', 0, 0, axis_index_groups=rings, tiled=True)  8.47 us
    pallas_call x2, Pallas kernels, slots(): pl.pallas_call(functools.partial(slot_kernel, scale, start), grid_spec=pl...  8.14 us
    pallas_call x1, Pallas kernels, spectra(): pl.pallas_call(spectrum_kernel, grid=(count // step,), in_specs=[pl.Block...  6.82 us
    ppermute x6, waiting for transfers between devices, to_y(): lax.ppermute(covs[dy], 'dp', [(i, i ^ dy * NZ) for i in range(NY * NZ)])  6.73 us
    pallas_call x1, Pallas kernels, project(): pl.pallas_call(project_kernel, grid=(GROUPS,), in_specs=[pl.BlockSpec(hel...  5.93 us
  transfers between devices with their start and end apart: 16, of which 9 were waited for; matrix products, arithmetic and copies ran while one was open for 0% of the time, Pallas kernels for 15%

profile of v2, /device:TPU:24, one launch (start us, length us, event | category | flops | bytes accessed | tf_op | source)
XLA Modules:
  0.0 96.9 jit_solution(17575262583159435443)
XLA Ops:
  0.6 0.0 copy-start
  0.6 0.0 copy-start.1
  0.7 6.8 %spectra.1 = (bf16[32,48,128]{2,1,0:T(8,128)(2,1)S(1)}, bf16[32,48,128]{2,1,0:T(8,128)(2,1)S(1)}, bf16[32,64,128]{2,1,0:T(8,128)(2,1)S(1)}, bf16[32,64,128]{2,1,...) custom-call(bf16[32,128,512]{2,1,0:T(8,128)(2,1)} %x_ref.1, ...), custom_call_target="tpu_custom_call" | custom-call | flops 2684354560 | bytes 8388608 | tf_op jit(solution)/shard_map/spectra/pallas_call | solution.py:91
  7.5 3.1 %collective-permute-start = (bf16[32,48,128]{2,1,0:T(8,128)(2,1)S(1)}, bf16[32,48,128]{2,1,0:T(8,128)(2,1)S(1)}, u32[]{:S(2)}, u32[]{:S(2)}) collective-permute-start(bf16[32,48,128]{2,1,0:T(8,128)(2,1)S(1)} %get-tuple-element.28), channel_id=1, source_target_pairs={{0,4},{1,5},{2,6},{3,7},{4,0},{5,1},{6,2},{7,3},{8,12},{9,13},{10,... | collective-permute-start | bytes 1179656 | tf_op jit(solution)/shard_map/ppermute | solution.py:261
  10.6 0.0 collective-permute-start.1
  10.6 1.2 %collective-permute-start.2 = (bf16[32,64,128]{2,1,0:T(8,128)(2,1)S(1)}, bf16[32,64,128]{2,1,0:T(8,128)(2,1)S(1)}, u32[]{:S(2)}, u32[]{:S(2)}) collective-permute-start(bf16[32,64,128]{2,1,0:T(8,128)(2,1)S(1)} %get-tuple-element.32), channel_id=1, source_target_pairs={{0,2},{1,3},{2,0},{3,1},{4,6},{5,7},{6,4},{7,5},{8,10},{9,11},{10,... | collective-permute-start | bytes 1572872 | tf_op jit(solution)/shard_map/ppermute | solution.py:261
  11.8 2.1 %collective-permute-start.3 = (bf16[32,64,128]{2,1,0:T(8,128)(2,1)S(1)}, bf16[32,64,128]{2,1,0:T(8,128)(2,1)S(1)}, u32[]{:S(2)}, u32[]{:S(2)}) collective-permute-start(bf16[32,64,128]{2,1,0:T(8,128)(2,1)S(1)} %get-tuple-element.33), channel_id=1, source_target_pairs={{0,6},{1,7},{2,4},{3,5},{4,2},{5,3},{6,0},{7,1},{8,14},{9,15},{10,... | collective-permute-start | bytes 1572872 | tf_op jit(solution)/shard_map/ppermute | solution.py:261
  13.8 0.6 collective-permute-start.4
  14.4 6.7 %collective-permute-done.refs_0_ = bf16[32,48,128]{2,1,0:T(8,128)(2,1)S(1)} collective-permute-done((bf16[32,48,128]{2,1,0:T(8,128)(2,1)S(1)}, bf16[32,48,128]{2,1,0:T(8,128)(2,1)S(1)}, u32[]{:S(2)}, u32[]{:S(2)}) %collective-permute-start) | collective-permute-done | bytes 393248 | tf_op jit(solution)/shard_map/ppermute | solution.py:261
  21.2 0.1 collective-permute-start.5
  21.3 7.3 %collective-permute-done.1.refs_1_ = bf16[32,48,128]{2,1,0:T(8,128)(2,1)S(1)} collective-permute-done((bf16[32,48,128]{2,1,0:T(8,128)(2,1)S(1)}, bf16[32,48,128]{2,1,0:T(8,128)(2,1)S(1)}, u32[]{:S(2)}, u32[]{:S(2)}) %collective-permute-start.1) | collective-permute-done | bytes 393248 | tf_op jit(solution)/shard_map/ppermute | solution.py:261
  28.6 0.8 collective-permute-start.6
  29.4 11.5 %collective-permute-done.2.refs_2_ = bf16[32,64,128]{2,1,0:T(8,128)(2,1)S(1)} collective-permute-done((bf16[32,64,128]{2,1,0:T(8,128)(2,1)S(1)}, bf16[32,64,128]{2,1,0:T(8,128)(2,1)S(1)}, u32[]{:S(2)}, u32[]{:S(2)}) %collective-permute-start.2) | collective-permute-done | bytes 524320 | tf_op jit(solution)/shard_map/ppermute | solution.py:261
  40.9 2.0 %collective-permute-start.10 = (bf16[32,16,128]{2,1,0:T(8,128)(2,1)S(1)}, bf16[32,16,128]{2,1,0:T(8,128)(2,1)S(1)}, u32[]{:S(2)}, u32[]{:S(2)}) collective-permute-start(bf16[32,16,128]{2,1,0:T(8,128)(2,1)S(1)} %get-tuple-element.42), channel_id=1, source_target_pairs={{0,4},{1,5},{2,6},{3,7},{4,0},{5,1},{6,2},{7,3},{8,12},{9,13},{10,... | collective-permute-start | bytes 393224 | tf_op jit(solution)/shard_map/ppermute | solution.py:261
  42.9 0.0 collective-permute-done.3.refs_3_
  42.9 0.0 collective-permute-start.11
  42.9 8.2 %collective-permute-done.4.refs_4_ = bf16[32,64,128]{2,1,0:T(8,128)(2,1)S(1)} collective-permute-done((bf16[32,64,128]{2,1,0:T(8,128)(2,1)S(1)}, bf16[32,64,128]{2,1,0:T(8,128)(2,1)S(1)}, u32[]{:S(2)}, u32[]{:S(2)}) %collective-permute-start.4) | collective-permute-done | bytes 524320 | tf_op jit(solution)/shard_map/ppermute | solution.py:261
  51.1 0.8 collective-permute-done.5.refs_5_
  51.9 0.0 collective-permute-done.6.refs_6_
  51.9 0.0 copy-done
  51.9 0.0 copy-done.1
  51.9 5.6 %slots.2 = (bf16[2,4,6,256,128]{4,3,2,1,0:T(8,128)(2,1)}, bf16[6,128,128]{2,1,0:T(8,128)(2,1)S(1)}, bf16[6,128,128]{2,1,0:T(8,128)(2,1)S(1)}, bf16[6,128,128]{2,1,0:T(8,128)(2,1)S(1)}, bf16[6,128,128]{2,1,0:T(8,128)(2,1)S(1)}) custom-call(s32[32]{0:T(128)S(1)} %copy-done.1, bf16[32,48,128]{2,1,0:T(8,128)(2,1)S(1)} %collective-permute-done.refs_0_, ...), custom_call_target="tpu_custom_call" | custom-call | flops 4831838208 | bytes 9437184 | tf_op jit(solution)/shard_map/slots/pallas_call | solution.py:161
  57.4 0.8 collective-permute-start.7
  58.2 2.5 %collective-permute-start.8 = (bf16[6,128,128]{2,1,0:T(8,128)(2,1)S(1)}, bf16[6,128,128]{2,1,0:T(8,128)(2,1)S(1)}, u32[]{:S(2)}, u32[]{:S(2)}) collective-permute-start(bf16[6,128,128]{2,1,0:T(8,128)(2,1)S(1)} %get-tuple-element.40), channel_id=1, source_target_pairs={{0,128},{8,136},{16,144},{24,152},{32,160},{40,168},{48,176},{56,1... | collective-permute-start | bytes 589832 | tf_op jit(solution)/shard_map/ppermute | solution.py:267
  60.7 1.5 %collective-permute-start.9 = (bf16[6,128,128]{2,1,0:T(8,128)(2,1)S(1)}, bf16[6,128,128]{2,1,0:T(8,128)(2,1)S(1)}, u32[]{:S(2)}, u32[]{:S(2)}) collective-permute-start(bf16[6,128,128]{2,1,0:T(8,128)(2,1)S(1)} %get-tuple-element.41), channel_id=1, source_target_pairs={{0,192},{8,200},{16,208},{24,216},{32,224},{40,232},{48,240},{56,2... | collective-permute-start | bytes 589832 | tf_op jit(solution)/shard_map/ppermute | solution.py:267
  62.2 0.0 collective-permute-done.10.refs_0_
  62.2 0.0 collective-permute-done.11.refs_1_
  62.2 2.6 %slots.3 = (bf16[2,4,2,256,128]{4,3,2,1,0:T(8,128)(2,1)}, bf16[2,128,128]{2,1,0:T(8,128)(2,1)S(1)}, bf16[2,128,128]{2,1,0:T(8,128)(2,1)S(1)}, bf16[2,128,128]{2,1,0:T(8,128)(2,1)S(1)}, bf16[2,128,128]{2,1,0:T(8,128)(2,1)S(1)}) custom-call(s32[32]{0:T(128)S(1)} %copy-done.1, bf16[32,16,128]{2,1,0:T(8,128)(2,1)S(1)} %collective-permute-done.10.refs_0_, ...), custom_call_target="tpu_custom_call" | custom-call | flops 1610612736 | bytes 3145728 | tf_op jit(solution)/shard_map/slots/pallas_call | solution.py:161
  64.7 0.0 collective-permute-start.12
  64.8 3.2 %collective-permute-start.13 = (bf16[2,128,128]{2,1,0:T(8,128)(2,1)S(1)}, bf16[2,128,128]{2,1,0:T(8,128)(2,1)S(1)}, u32[]{:S(2)}, u32[]{:S(2)}) collective-permute-start(bf16[2,128,128]{2,1,0:T(8,128)(2,1)S(1)} %get-tuple-element.46), channel_id=1, source_target_pairs={{0,128},{8,136},{16,144},{24,152},{32,160},{40,168},{48,176},{56,1... | collective-permute-start | bytes 196616 | tf_op jit(solution)/shard_map/ppermute | solution.py:267
  68.0 2.9 %collective-permute-done.12.refs_5_ = bf16[2,128,128]{2,1,0:T(8,128)(2,1)S(1)} collective-permute-done((bf16[2,128,128]{2,1,0:T(8,128)(2,1)S(1)}, bf16[2,128,128]{2,1,0:T(8,128)(2,1)S(1)}, u32[]{:S(2)}, u32[]{:S(2)}) %collective-permute-start.12) | collective-permute-done | bytes 65568 | tf_op jit(solution)/shard_map/ppermute | solution.py:267
  70.8 1.6 %collective-permute-start.14 = (bf16[2,128,128]{2,1,0:T(8,128)(2,1)S(1)}, bf16[2,128,128]{2,1,0:T(8,128)(2,1)S(1)}, u32[]{:S(2)}, u32[]{:S(2)}) collective-permute-start(bf16[2,128,128]{2,1,0:T(8,128)(2,1)S(1)} %get-tuple-element.47), channel_id=1, source_target_pairs={{0,192},{8,200},{16,208},{24,216},{32,224},{40,232},{48,240},{56,2... | collective-permute-start | bytes 196616 | tf_op jit(solution)/shard_map/ppermute | solution.py:267
  72.5 0.2 collective-permute-done.13.refs_6_
  72.7 3.6 %collective-permute-done.14.refs_7_ = bf16[2,128,128]{2,1,0:T(8,128)(2,1)S(1)} collective-permute-done((bf16[2,128,128]{2,1,0:T(8,128)(2,1)S(1)}, bf16[2,128,128]{2,1,0:T(8,128)(2,1)S(1)}, u32[]{:S(2)}, u32[]{:S(2)}) %collective-permute-start.14) | collective-permute-done | bytes 65568 | tf_op jit(solution)/shard_map/ppermute | solution.py:267
  76.3 0.0 collective-permute-done.7.refs_1_
  76.3 0.0 collective-permute-done.8.refs_2_
  76.3 0.0 collective-permute-done.9.refs_3_
  76.3 0.9 join.1
  77.2 8.5 %all-to-all-start = ((bf16[8,128,128]{2,1,0:T(8,128)(2,1)}), bf16[8,128,128]{2,1,0:T(8,128)(2,1)S(1)}, u32[]{:S(2)}, u32[]{:S(2)}) async-start(bf16[8,128,128]{2,1,0:T(8,128)(2,1)} %join.1), calls=%async_computation | async-start | bytes 524288 | tf_op jit(solution)/shard_map/all_to_all | solution.py:290
  85.7 5.9 %project.1 = bf16[2,4,8,256,128]{4,3,2,1,0:T(8,128)(2,1)} custom-call(bf16[2,4,6,256,128]{4,3,2,1,0:T(8,128)(2,1)} %get-tuple-element.48.first_ref, bf16[2,4,2,256,128]{4,3,2,1,0:T(8,128)(2,1)} %get-tuple-element.49.second_ref, bf16[4,8,128,128]{3,2,1,0:T(8,128)(2,1)} %bitcast.8), custom_call_target="tpu_custom_call" | custom-call | flops 536870912 | bytes 9437184 | tf_op jit(solution)/shard_map/project/pallas_call | solution.py:209
  91.6 4.6 %all-to-all-done.parts_ref = bf16[8,128,128]{2,1,0:T(8,128)(2,1)S(1)} async-done(((bf16[8,128,128]{2,1,0:T(8,128)(2,1)}), bf16[8,128,128]{2,1,0:T(8,128)(2,1)S(1)}, u32[]{:S(2)}, u32[]{:S(2)}) %all-to-all-start) | async-done | bytes 262176 | tf_op jit(solution)/shard_map/all_to_all | solution.py:290
  96.1 0.8 finish.1
Async XLA Ops:
  0.6 51.2 %copy-start = (bf16[32,128,128]{2,1,0:T(8,128)(2,1)S(1)}, bf16[32,128,128]{2,1,0:T(8,128)(2,1)}, u32[]{:S(2)}) copy-start(bf16[32,128,128]{2,1,0:T(8,128)(2,1)} %param.11) | copy-start | bytes 3145732
  0.6 51.2 %copy-start.1 = (s32[32]{0:T(128)S(1)}, s32[32]{0:T(128)}, u32[]{:S(2)}) copy-start(s32[32]{0:T(128)} %counts_ref.3) | copy-start | bytes 388
  7.5 13.7 %collective-permute-start = (bf16[32,48,128]{2,1,0:T(8,128)(2,1)S(1)}, bf16[32,48,128]{2,1,0:T(8,128)(2,1)S(1)}, u32[]{:S(2)}, u32[]{:S(2)}) collective-permute-start(bf16[32,48,128]{2,1,0:T(8,128)(2,1)S(1)} %get-tuple-element.28), channel_id=1, source_target_pairs={{0,4},{1,5},{2,6},{3,7},{4,0},{5,1},{6,2},{7,3},{8,12},{9,13},{10,... | collective-permute-start | bytes 1179656 | tf_op jit(solution)/shard_map/ppermute | solution.py:261
  10.6 18.0 %collective-permute-start.1 = (bf16[32,48,128]{2,1,0:T(8,128)(2,1)S(1)}, bf16[32,48,128]{2,1,0:T(8,128)(2,1)S(1)}, u32[]{:S(2)}, u32[]{:S(2)}) collective-permute-start(bf16[32,48,128]{2,1,0:T(8,128)(2,1)S(1)} %get-tuple-element.29), channel_id=1, source_target_pairs={{0,5},{1,4},{2,7},{3,6},{4,1},{5,0},{6,3},{7,2},{8,13},{9,12},{10,... | collective-permute-start | bytes 1179656 | tf_op jit(solution)/shard_map/ppermute | solution.py:261
  10.6 30.3 %collective-permute-start.2 = (bf16[32,64,128]{2,1,0:T(8,128)(2,1)S(1)}, bf16[32,64,128]{2,1,0:T(8,128)(2,1)S(1)}, u32[]{:S(2)}, u32[]{:S(2)}) collective-permute-start(bf16[32,64,128]{2,1,0:T(8,128)(2,1)S(1)} %get-tuple-element.32), channel_id=1, source_target_pairs={{0,2},{1,3},{2,0},{3,1},{4,6},{5,7},{6,4},{7,5},{8,10},{9,11},{10,... | collective-permute-start | bytes 1572872 | tf_op jit(solution)/shard_map/ppermute | solution.py:261
  11.8 31.1 %collective-permute-start.3 = (bf16[32,64,128]{2,1,0:T(8,128)(2,1)S(1)}, bf16[32,64,128]{2,1,0:T(8,128)(2,1)S(1)}, u32[]{:S(2)}, u32[]{:S(2)}) collective-permute-start(bf16[32,64,128]{2,1,0:T(8,128)(2,1)S(1)} %get-tuple-element.33), channel_id=1, source_target_pairs={{0,6},{1,7},{2,4},{3,5},{4,2},{5,3},{6,0},{7,1},{8,14},{9,15},{10,... | collective-permute-start | bytes 1572872 | tf_op jit(solution)/shard_map/ppermute | solution.py:261
  13.8 37.2 %collective-permute-start.4 = (bf16[32,64,128]{2,1,0:T(8,128)(2,1)S(1)}, bf16[32,64,128]{2,1,0:T(8,128)(2,1)S(1)}, u32[]{:S(2)}, u32[]{:S(2)}) collective-permute-start(bf16[32,64,128]{2,1,0:T(8,128)(2,1)S(1)} %get-tuple-element.34), channel_id=1, source_target_pairs={{0,3},{1,2},{2,1},{3,0},{4,7},{5,6},{6,5},{7,4},{8,11},{9,10},{10,... | collective-permute-start | bytes 1572872 | tf_op jit(solution)/shard_map/ppermute | solution.py:261
  21.2 30.7 %collective-permute-start.5 = (bf16[32,64,128]{2,1,0:T(8,128)(2,1)S(1)}, bf16[32,64,128]{2,1,0:T(8,128)(2,1)S(1)}, u32[]{:S(2)}, u32[]{:S(2)}) collective-permute-start(bf16[32,64,128]{2,1,0:T(8,128)(2,1)S(1)} %get-tuple-element.35), channel_id=1, source_target_pairs={{0,7},{1,6},{2,5},{3,4},{4,3},{5,2},{6,1},{7,0},{8,15},{9,14},{10,... | collective-permute-start | bytes 1572872 | tf_op jit(solution)/shard_map/ppermute | solution.py:261
  28.6 23.3 %collective-permute-start.6 = (bf16[32,64,128]{2,1,0:T(8,128)(2,1)S(1)}, bf16[32,64,128]{2,1,0:T(8,128)(2,1)S(1)}, u32[]{:S(2)}, u32[]{:S(2)}) collective-permute-start(bf16[32,64,128]{2,1,0:T(8,128)(2,1)S(1)} %get-tuple-element.36), channel_id=1, source_target_pairs={{0,1},{1,0},{2,3},{3,2},{4,5},{5,4},{6,7},{7,6},{8,9},{9,8},{10,11... | collective-permute-start | bytes 1572872 | tf_op jit(solution)/shard_map/ppermute | solution.py:261
  40.9 21.3 %collective-permute-start.10 = (bf16[32,16,128]{2,1,0:T(8,128)(2,1)S(1)}, bf16[32,16,128]{2,1,0:T(8,128)(2,1)S(1)}, u32[]{:S(2)}, u32[]{:S(2)}) collective-permute-start(bf16[32,16,128]{2,1,0:T(8,128)(2,1)S(1)} %get-tuple-element.42), channel_id=1, source_target_pairs={{0,4},{1,5},{2,6},{3,7},{4,0},{5,1},{6,2},{7,3},{8,12},{9,13},{10,... | collective-permute-start | bytes 393224 | tf_op jit(solution)/shard_map/ppermute | solution.py:261
  42.9 19.3 %collective-permute-start.11 = (bf16[32,16,128]{2,1,0:T(8,128)(2,1)S(1)}, bf16[32,16,128]{2,1,0:T(8,128)(2,1)S(1)}, u32[]{:S(2)}, u32[]{:S(2)}) collective-permute-start(bf16[32,16,128]{2,1,0:T(8,128)(2,1)S(1)} %get-tuple-element.43), channel_id=1, source_target_pairs={{0,5},{1,4},{2,7},{3,6},{4,1},{5,0},{6,3},{7,2},{8,13},{9,12},{10,... | collective-permute-start | bytes 393224 | tf_op jit(solution)/shard_map/ppermute | solution.py:261
  57.4 18.9 %collective-permute-start.7 = (bf16[6,128,128]{2,1,0:T(8,128)(2,1)S(1)}, bf16[6,128,128]{2,1,0:T(8,128)(2,1)S(1)}, u32[]{:S(2)}, u32[]{:S(2)}) collective-permute-start(bf16[6,128,128]{2,1,0:T(8,128)(2,1)S(1)} %get-tuple-element.39), channel_id=1, source_target_pairs={{0,64},{8,72},{16,80},{24,88},{32,96},{40,104},{48,112},{56,120},{... | collective-permute-start | bytes 589832 | tf_op jit(solution)/shard_map/ppermute | solution.py:267
  58.2 18.1 %collective-permute-start.8 = (bf16[6,128,128]{2,1,0:T(8,128)(2,1)S(1)}, bf16[6,128,128]{2,1,0:T(8,128)(2,1)S(1)}, u32[]{:S(2)}, u32[]{:S(2)}) collective-permute-start(bf16[6,128,128]{2,1,0:T(8,128)(2,1)S(1)} %get-tuple-element.40), channel_id=1, source_target_pairs={{0,128},{8,136},{16,144},{24,152},{32,160},{40,168},{48,176},{56,1... | collective-permute-start | bytes 589832 | tf_op jit(solution)/shard_map/ppermute | solution.py:267
  60.7 15.7 %collective-permute-start.9 = (bf16[6,128,128]{2,1,0:T(8,128)(2,1)S(1)}, bf16[6,128,128]{2,1,0:T(8,128)(2,1)S(1)}, u32[]{:S(2)}, u32[]{:S(2)}) collective-permute-start(bf16[6,128,128]{2,1,0:T(8,128)(2,1)S(1)} %get-tuple-element.41), channel_id=1, source_target_pairs={{0,192},{8,200},{16,208},{24,216},{32,224},{40,232},{48,240},{56,2... | collective-permute-start | bytes 589832 | tf_op jit(solution)/shard_map/ppermute | solution.py:267
  64.7 6.1 %collective-permute-start.12 = (bf16[2,128,128]{2,1,0:T(8,128)(2,1)S(1)}, bf16[2,128,128]{2,1,0:T(8,128)(2,1)S(1)}, u32[]{:S(2)}, u32[]{:S(2)}) collective-permute-start(bf16[2,128,128]{2,1,0:T(8,128)(2,1)S(1)} %get-tuple-element.45), channel_id=1, source_target_pairs={{0,64},{8,72},{16,80},{24,88},{32,96},{40,104},{48,112},{56,120},{... | collective-permute-start | bytes 196616 | tf_op jit(solution)/shard_map/ppermute | solution.py:267
  64.8 7.9 %collective-permute-start.13 = (bf16[2,128,128]{2,1,0:T(8,128)(2,1)S(1)}, bf16[2,128,128]{2,1,0:T(8,128)(2,1)S(1)}, u32[]{:S(2)}, u32[]{:S(2)}) collective-permute-start(bf16[2,128,128]{2,1,0:T(8,128)(2,1)S(1)} %get-tuple-element.46), channel_id=1, source_target_pairs={{0,128},{8,136},{16,144},{24,152},{32,160},{40,168},{48,176},{56,1... | collective-permute-start | bytes 196616 | tf_op jit(solution)/shard_map/ppermute | solution.py:267
  70.8 5.5 %collective-permute-start.14 = (bf16[2,128,128]{2,1,0:T(8,128)(2,1)S(1)}, bf16[2,128,128]{2,1,0:T(8,128)(2,1)S(1)}, u32[]{:S(2)}, u32[]{:S(2)}) collective-permute-start(bf16[2,128,128]{2,1,0:T(8,128)(2,1)S(1)} %get-tuple-element.47), channel_id=1, source_target_pairs={{0,192},{8,200},{16,208},{24,216},{32,224},{40,232},{48,240},{56,2... | collective-permute-start | bytes 196616 | tf_op jit(solution)/shard_map/ppermute | solution.py:267
  77.2 19.0 %all-to-all-start = ((bf16[8,128,128]{2,1,0:T(8,128)(2,1)}), bf16[8,128,128]{2,1,0:T(8,128)(2,1)S(1)}, u32[]{:S(2)}, u32[]{:S(2)}) async-start(bf16[8,128,128]{2,1,0:T(8,128)(2,1)} %join.1), calls=%async_computation | async-start | bytes 524288 | tf_op jit(solution)/shard_map/all_to_all | solution.py:290

commit v3 on v2

--- a/solution.py
+++ b/solution.py
@@ -86,7 +86,7 @@
     count, radii, samples = images.shape
     nodes = interp.shape[1]
     total = assignment.shape[0]
-    step = 8
+    step = 16
     tables = jnp.asarray(angle_tables(samples, total))
     return pl.pallas_call(
         spectrum_kernel,
@@ -110,15 +110,17 @@
     )(*(in_hbm(x) for x in (images, interp, assignment[None, :], tables)))
 
 
-def slot_kernel(scale, start, counts_ref, *refs):
+def slot_kernel(scale, start, aliased, counts_ref, *refs):
     pieces, basis_ref = refs[:NO], refs[NO]
-    coef_ref, covs, turned = refs[NO + 1], refs[NO + 2 : NO + 2 + NY], refs[-1]
+    refs = refs[NO + 1 + aliased :]
+    coef_ref, covs, turned = refs[0], refs[1 : 1 + NY], refs[-1]
     me = lax.axis_index("order")
     y = lax.axis_index("dp") // NZ
     group = start + pl.program_id(0)
-    images, rows, nodes = pieces[0].shape
+    images, rows, nodes = pieces[0].shape[0], HEIGHT, pieces[0].shape[2]
     for i, d in enumerate(SPLIT + WHOLE):
-        turned[d] = jnp.swapaxes(pieces[i][...], 0, 1)
+        at = pl.multiple_of((group if d in WHOLE else group - start) * rows, rows)
+        turned[d] = jnp.swapaxes(pieces[i][:, pl.ds(at, rows), :], 0, 1)
     width = basis_ref.shape[3]
     lane = lax.broadcasted_iota(jnp.int32, (nodes, width), 1)
     row = lax.broadcasted_iota(jnp.int32, (width, width), 0)
@@ -128,7 +130,7 @@
         yy = y ^ dy
         for zl in range(2):
             limit = counts_ref[yy * NZ + group * 2 + zl]
-            basis = jnp.where(lane < limit, basis_ref[yy, zl], 0)
+            basis = jnp.where(lane < limit, basis_ref[yy, group * 2 + zl], 0)
             spec = jnp.concatenate(
                 [
                     turned[me ^ j, p * 8 + dy * 2 + zl]
@@ -150,26 +152,25 @@
             covs[dy][zl] = (jnp.where(upper, real, imag) * scale).astype(jnp.bfloat16)
 
 
-def slots(pieces, counts, basis, scale, start, groups):
+def slots(pieces, counts, basis, scale, start, groups, covs=()):
     images, _, nodes = pieces[0].shape
     _, _, _, width = basis.shape
     rows = HEIGHT
     total = NO * images
-    part = pl.BlockSpec((images, rows, nodes), lambda g, c: (0, g, 0))
-    whole = pl.BlockSpec((images, rows, nodes), lambda g, c: (0, start + g, 0))
-    weights = pl.BlockSpec((NY, 2, nodes, width), lambda g, c: (0, start + g, 0, 0))
     return pl.pallas_call(
-        functools.partial(slot_kernel, scale, start),
+        functools.partial(slot_kernel, scale, start, len(covs)),
         grid_spec=pltpu.PrefetchScalarGridSpec(
             num_scalar_prefetch=1,
             grid=(groups,),
-            in_specs=[part] * len(SPLIT) + [whole] * len(WHOLE) + [weights],
+            in_specs=[pl.BlockSpec(memory_space=pltpu.VMEM)] * (NO + 1)
+            + [pl.BlockSpec(memory_space=pl.ANY)] * len(covs),
             out_specs=[pl.BlockSpec((2, NY, 2, total, width), lambda g, c: (0, 0, g, 0, 0))]
-            + [pl.BlockSpec((2, width, width), lambda g, c: (g, 0, 0))] * NY,
+            + [pl.BlockSpec((2, width, width), lambda g, c: (start + g, 0, 0))] * NY,
             scratch_shapes=[pltpu.VMEM((NO, rows, images, nodes), jnp.bfloat16)],
         ),
         out_shape=[pltpu.HBM((2, NY, 2 * groups, total, width), jnp.bfloat16)]
-        + [jax.ShapeDtypeStruct((2 * groups, width, width), jnp.bfloat16)] * NY,
+        + [jax.ShapeDtypeStruct((NZ, width, width), jnp.bfloat16)] * NY,
+        input_output_aliases={NO + 2 + i: 1 + i for i in range(len(covs))},
         compiler_params=pltpu.CompilerParams(vmem_limit_bytes=32 << 20),
         cost_estimate=pl.CostEstimate(
             flops=groups * 64 * 6 * total * nodes * width,
@@ -177,7 +178,7 @@
             transcendentals=0,
         ),
         name="slots",
-    )(counts, *pieces, basis)
+    )(counts, *pieces, basis, *covs)
 
 
 def project_kernel(first_ref, second_ref, eigen_ref, out_ref):
@@ -225,15 +226,10 @@
 
 
 def join_kernel(*refs):
-    ins, out_ref = refs[:-1], refs[-1]
-    done = 0
-    for part in (ins[:NY], ins[NY:]):
-        held = part[0].shape[0]
-        added = part[0][...].astype(jnp.float32)
-        for moved in part[1:]:
-            added += moved[...].astype(jnp.float32)
-        out_ref[done : done + held] = added.astype(jnp.bfloat16)
-        done += held
+    added = refs[0][...].astype(jnp.float32)
+    for moved in refs[1:-1]:
+        added += moved[...].astype(jnp.float32)
+    refs[-1][...] = added.astype(jnp.bfloat16)
 
 
 def finish_kernel(parts_ref, out_ref):
@@ -265,7 +261,7 @@
     def to_y(covs):
         return [
             lax.ppermute(covs[dy], "dp", [(i, i ^ (dy * NZ)) for i in range(NY * NZ)])
-            for dy in range(1, NY)
+            for dy in (2, 1, 3)
         ]
 
     scale = 1.0 / total
@@ -275,17 +271,15 @@
     *gated, first[0], first[1] = lax.optimization_barrier(tuple(pieces[near:]) + tuple(first))
     second = exchange(gated, SPLIT) + whole
     first += whole
-    coef_first, *cov_first = slots(first, counts, basis, scale, 0, FIRST)
-    moved_first = to_y(cov_first)
-    coef_second, *cov_second = slots(second, counts, basis, scale, FIRST, GROUPS - FIRST)
-    moved_second = to_y(cov_second)
+    coef_first, *covs = slots(first, counts, basis, scale, 0, FIRST)
+    coef_second, *covs = slots(second, counts, basis, scale, FIRST, GROUPS - FIRST, covs)
     projected = project(coef_first, coef_second, eigen)
     parts = pl.pallas_call(
         join_kernel,
         out_shape=jax.ShapeDtypeStruct((NZ, width, width), jnp.bfloat16),
         compiler_params=pltpu.CompilerParams(vmem_limit_bytes=8 << 20),
         name="join",
-    )(cov_first[0], *moved_first, cov_second[0], *moved_second)
+    )(covs[0], *to_y(covs))
     rings = [[y * NZ + z for z in range(NZ)] for y in range(NY)]
     parts = lax.all_to_all(parts, "dp", 0, 0, axis_index_groups=rings, tiled=True)
     covariance = pl.pallas_call(

time: 98.2 us -> 97.7 us (level); the launches traced: 96.9 us -> 97.4 us
  waiting for transfers between devices: 45.8 us -> 52.2 us
  starting transfers between devices: 27.9 us -> 22.4 us
    ppermute x6 -> x3, starting transfers between devices: 9.56 us -> 4.09 us  [to_y(): lax.ppermute(covs[dy], 'dp', [(i, i ^ dy * NZ) for i in range(NY * NZ)])]
    ppermute x6 -> x3, waiting for transfers between devices: 6.73 us -> 11.6 us  [to_y(): lax.ppermute(covs[dy], 'dp', [(i, i ^ dy * NZ) for i in range(NY * NZ)])]
    all_to_all x1, waiting for transfers between devices: 4.55 us -> 6.13 us  [body(): lax.all_to_all(parts, 'dp', 0, 0, axis_index_groups=rings, tiled=True)]
  transfers between devices with their start and end apart: 16 -> 13, of which waited for: 9 -> 9; matrix products, arithmetic and copies ran while one was open for 0% -> 0% of each run, Pallas kernels for 15% -> 12%
where the time goes in v3:
time: 97.7 us; the launch traced here: 97.4 us
  waiting for transfers between devices  52.2 us (53%)
  starting transfers between devices  22.4 us (23%)
  Pallas kernels  22.1 us (23%)
    ppermute x9, waiting for transfers between devices, exchange(): lax.ppermute(piece, 'order', [(i, i ^ d) for i in range(NO)])  34.5 us
    ppermute x3, waiting for transfers between devices, to_y(): lax.ppermute(covs[dy], 'dp', [(i, i ^ dy * NZ) for i in range(NY * NZ)])  11.6 us
    ppermute x9, starting transfers between devices, exchange(): lax.ppermute(piece, 'order', [(i, i ^ d) for i in range(NO)])  9.88 us
    all_to_all x1, starting transfers between devices, body(): lax.all_to_all(parts, 'dp', 0, 0, axis_index_groups=rings, tiled=True)  8.46 us
    pallas_call x2, Pallas kernels, slots(): pl.pallas_call(functools.partial(slot_kernel, scale, start, len(covs)), g...  7.87 us
    pallas_call x1, Pallas kernels, spectra(): pl.pallas_call(spectrum_kernel, grid=(count // step,), in_specs=[pl.Block...  6.64 us
    all_to_all x1, waiting for transfers between devices, body(): lax.all_to_all(parts, 'dp', 0, 0, axis_index_groups=rings, tiled=True)  6.13 us
    pallas_call x1, Pallas kernels, project(): pl.pallas_call(project_kernel, grid=(GROUPS,), in_specs=[pl.BlockSpec(hel...  5.94 us
  transfers between devices with their start and end apart: 13, of which 9 were waited for; matrix products, arithmetic and copies ran while one was open for 0% of the time, Pallas kernels for 12%

profile of v3, /device:TPU:24, one launch (start us, length us, event | category | flops | bytes accessed | tf_op | source)
XLA Modules:
  0.0 97.4 jit_solution(2509953856088533706)
XLA Ops:
  0.6 0.0 copy-start
  0.6 0.0 copy-start.1
  0.7 6.6 %spectra.1 = (bf16[32,48,128]{2,1,0:T(8,128)(2,1)S(1)}, bf16[32,48,128]{2,1,0:T(8,128)(2,1)S(1)}, bf16[32,64,128]{2,1,0:T(8,128)(2,1)S(1)}, bf16[32,64,128]{2,1,...) custom-call(bf16[32,128,512]{2,1,0:T(8,128)(2,1)} %x_ref.1, ...), custom_call_target="tpu_custom_call" | custom-call | flops 2684354560 | bytes 8388608 | tf_op jit(solution)/shard_map/spectra/pallas_call | solution.py:91
  7.3 3.1 %collective-permute-start = (bf16[32,48,128]{2,1,0:T(8,128)(2,1)S(1)}, bf16[32,48,128]{2,1,0:T(8,128)(2,1)S(1)}, u32[]{:S(2)}, u32[]{:S(2)}) collective-permute-start(bf16[32,48,128]{2,1,0:T(8,128)(2,1)S(1)} %get-tuple-element.28), channel_id=1, source_target_pairs={{0,4},{1,5},{2,6},{3,7},{4,0},{5,1},{6,2},{7,3},{8,12},{9,13},{10,... | collective-permute-start | bytes 1179656 | tf_op jit(solution)/shard_map/ppermute | solution.py:257
  10.4 0.0 collective-permute-start.1
  10.4 1.2 %collective-permute-start.4 = (bf16[32,64,128]{2,1,0:T(8,128)(2,1)S(1)}, bf16[32,64,128]{2,1,0:T(8,128)(2,1)S(1)}, u32[]{:S(2)}, u32[]{:S(2)}) collective-permute-start(bf16[32,64,128]{2,1,0:T(8,128)(2,1)S(1)} %get-tuple-element.32), channel_id=1, source_target_pairs={{0,2},{1,3},{2,0},{3,1},{4,6},{5,7},{6,4},{7,5},{8,10},{9,11},{10,... | collective-permute-start | bytes 1572872 | tf_op jit(solution)/shard_map/ppermute | solution.py:257
  11.6 2.1 %collective-permute-start.5 = (bf16[32,64,128]{2,1,0:T(8,128)(2,1)S(1)}, bf16[32,64,128]{2,1,0:T(8,128)(2,1)S(1)}, u32[]{:S(2)}, u32[]{:S(2)}) collective-permute-start(bf16[32,64,128]{2,1,0:T(8,128)(2,1)S(1)} %get-tuple-element.33), channel_id=1, source_target_pairs={{0,6},{1,7},{2,4},{3,5},{4,2},{5,3},{6,0},{7,1},{8,14},{9,15},{10,... | collective-permute-start | bytes 1572872 | tf_op jit(solution)/shard_map/ppermute | solution.py:257
  13.7 0.6 collective-permute-start.6
  14.3 6.7 %collective-permute-done.refs_0_ = bf16[32,48,128]{2,1,0:T(8,128)(2,1)S(1)} collective-permute-done((bf16[32,48,128]{2,1,0:T(8,128)(2,1)S(1)}, bf16[32,48,128]{2,1,0:T(8,128)(2,1)S(1)}, u32[]{:S(2)}, u32[]{:S(2)}) %collective-permute-start) | collective-permute-done | bytes 393248 | tf_op jit(solution)/shard_map/ppermute | solution.py:257
  21.0 0.1 collective-permute-start.7
  21.1 7.3 %collective-permute-done.1.refs_1_ = bf16[32,48,128]{2,1,0:T(8,128)(2,1)S(1)} collective-permute-done((bf16[32,48,128]{2,1,0:T(8,128)(2,1)S(1)}, bf16[32,48,128]{2,1,0:T(8,128)(2,1)S(1)}, u32[]{:S(2)}, u32[]{:S(2)}) %collective-permute-start.1) | collective-permute-done | bytes 393248 | tf_op jit(solution)/shard_map/ppermute | solution.py:257
  28.4 0.8 collective-permute-start.8
  29.2 11.5 %collective-permute-done.4.refs_2_ = bf16[32,64,128]{2,1,0:T(8,128)(2,1)S(1)} collective-permute-done((bf16[32,64,128]{2,1,0:T(8,128)(2,1)S(1)}, bf16[32,64,128]{2,1,0:T(8,128)(2,1)S(1)}, u32[]{:S(2)}, u32[]{:S(2)}) %collective-permute-start.4) | collective-permute-done | bytes 524320 | tf_op jit(solution)/shard_map/ppermute | solution.py:257
  40.7 2.0 %collective-permute-start.2 = (bf16[32,16,128]{2,1,0:T(8,128)(2,1)S(1)}, bf16[32,16,128]{2,1,0:T(8,128)(2,1)S(1)}, u32[]{:S(2)}, u32[]{:S(2)}) collective-permute-start(bf16[32,16,128]{2,1,0:T(8,128)(2,1)S(1)} %get-tuple-element.30), channel_id=1, source_target_pairs={{0,4},{1,5},{2,6},{3,7},{4,0},{5,1},{6,2},{7,3},{8,12},{9,13},{10,... | collective-permute-start | bytes 393224 | tf_op jit(solution)/shard_map/ppermute | solution.py:257
  42.7 0.0 collective-permute-done.5.refs_3_
  42.7 0.0 collective-permute-start.3
  42.7 8.2 %collective-permute-done.6.refs_4_ = bf16[32,64,128]{2,1,0:T(8,128)(2,1)S(1)} collective-permute-done((bf16[32,64,128]{2,1,0:T(8,128)(2,1)S(1)}, bf16[32,64,128]{2,1,0:T(8,128)(2,1)S(1)}, u32[]{:S(2)}, u32[]{:S(2)}) %collective-permute-start.6) | collective-permute-done | bytes 524320 | tf_op jit(solution)/shard_map/ppermute | solution.py:257
  50.9 0.8 collective-permute-done.7.refs_5_
  51.7 0.0 collective-permute-done.8.refs_6_
  51.7 0.0 copy-done
  51.7 0.0 copy-done.1
  51.7 5.3 %slots.2 = (bf16[2,4,6,256,128]{4,3,2,1,0:T(8,128)(2,1)}, bf16[8,128,128]{2,1,0:T(8,128)(2,1)S(1)}, bf16[8,128,128]{2,1,0:T(8,128)(2,1)S(1)}, bf16[8,128,128]{2,1,0:T(8,128)(2,1)S(1)}, bf16[8,128,128]{2,1,0:T(8,128)(2,1)S(1)}) custom-call(s32[32]{0:T(128)S(1)} %copy-done.1, bf16[32,48,128]{2,1,0:T(8,128)(2,1)S(1)} %collective-permute-done.refs_0_, ...), custom_call_target="tpu_custom_call" | custom-call | flops 4831838208 | bytes 9437184 | tf_op jit(solution)/shard_map/slots/pallas_call | solution.py:160
  57.0 0.0 collective-permute-done.2.refs_0_
  57.0 0.0 collective-permute-done.3.refs_1_
  57.0 2.6 %slots.3 = (bf16[2,4,2,256,128]{4,3,2,1,0:T(8,128)(2,1)}, bf16[8,128,128]{2,1,0:T(8,128)(2,1)S(1)}, bf16[8,128,128]{2,1,0:T(8,128)(2,1)S(1)}, bf16[8,128,128]{2,1,0:T(8,128)(2,1)S(1)}, bf16[8,128,128]{2,1,0:T(8,128)(2,1)S(1)}) custom-call(s32[32]{0:T(128)S(1)} %copy-done.1, ...), custom_call_target="tpu_custom_call", output_to_operand_aliasing={{1}: (10, {}), {2}: (11, {}), {3}: (12, {}), {4}: (13, {})} | custom-call | flops 1610612736 | bytes 3145728 | tf_op jit(solution)/shard_map/slots/pallas_call | solution.py:160
  59.6 1.2 %collective-permute-start.9 = (bf16[8,128,128]{2,1,0:T(8,128)(2,1)S(1)}, bf16[8,128,128]{2,1,0:T(8,128)(2,1)S(1)}, u32[]{:S(2)}, u32[]{:S(2)}) collective-permute-start(bf16[8,128,128]{2,1,0:T(8,128)(2,1)S(1)} %get-tuple-element.45), channel_id=1, source_target_pairs={{0,128},{8,136},{16,144},{24,152},{32,160},{40,168},{48,176},{56,1... | collective-permute-start | bytes 786440 | tf_op jit(solution)/shard_map/ppermute | solution.py:263
  60.8 1.4 %collective-permute-start.10 = (bf16[8,128,128]{2,1,0:T(8,128)(2,1)S(1)}, bf16[8,128,128]{2,1,0:T(8,128)(2,1)S(1)}, u32[]{:S(2)}, u32[]{:S(2)}) collective-permute-start(bf16[8,128,128]{2,1,0:T(8,128)(2,1)S(1)} %get-tuple-element.46), channel_id=1, source_target_pairs={{0,64},{8,72},{16,80},{24,88},{32,96},{40,104},{48,112},{56,120},{... | collective-permute-start | bytes 786440 | tf_op jit(solution)/shard_map/ppermute | solution.py:263
  62.2 1.5 %collective-permute-start.11 = (bf16[8,128,128]{2,1,0:T(8,128)(2,1)S(1)}, bf16[8,128,128]{2,1,0:T(8,128)(2,1)S(1)}, u32[]{:S(2)}, u32[]{:S(2)}) collective-permute-start(bf16[8,128,128]{2,1,0:T(8,128)(2,1)S(1)} %get-tuple-element.47), channel_id=1, source_target_pairs={{0,192},{8,200},{16,208},{24,216},{32,224},{40,232},{48,240},{56,2... | collective-permute-start | bytes 786440 | tf_op jit(solution)/shard_map/ppermute | solution.py:263
  63.7 6.6 %collective-permute-done.9.refs_1_ = bf16[8,128,128]{2,1,0:T(8,128)(2,1)S(1)} collective-permute-done((bf16[8,128,128]{2,1,0:T(8,128)(2,1)S(1)}, bf16[8,128,128]{2,1,0:T(8,128)(2,1)S(1)}, u32[]{:S(2)}, u32[]{:S(2)}) %collective-permute-start.9) | collective-permute-done | bytes 262176 | tf_op jit(solution)/shard_map/ppermute | solution.py:263
  70.3 3.9 %collective-permute-done.10.refs_2_ = bf16[8,128,128]{2,1,0:T(8,128)(2,1)S(1)} collective-permute-done((bf16[8,128,128]{2,1,0:T(8,128)(2,1)S(1)}, bf16[8,128,128]{2,1,0:T(8,128)(2,1)S(1)}, u32[]{:S(2)}, u32[]{:S(2)}) %collective-permute-start.10) | collective-permute-done | bytes 262176 | tf_op jit(solution)/shard_map/ppermute | solution.py:263
  74.1 1.1 %collective-permute-done.11.refs_3_ = bf16[8,128,128]{2,1,0:T(8,128)(2,1)S(1)} collective-permute-done((bf16[8,128,128]{2,1,0:T(8,128)(2,1)S(1)}, bf16[8,128,128]{2,1,0:T(8,128)(2,1)S(1)}, u32[]{:S(2)}, u32[]{:S(2)}) %collective-permute-start.11) | collective-permute-done | bytes 262176 | tf_op jit(solution)/shard_map/ppermute | solution.py:263
  75.3 0.8 join.1
  76.1 8.5 %all-to-all-start = ((bf16[8,128,128]{2,1,0:T(8,128)(2,1)}), bf16[8,128,128]{2,1,0:T(8,128)(2,1)S(1)}, u32[]{:S(2)}, u32[]{:S(2)}) async-start(bf16[8,128,128]{2,1,0:T(8,128)(2,1)} %join.1), calls=%async_computation | async-start | bytes 524288 | tf_op jit(solution)/shard_map/all_to_all | solution.py:284
  84.6 5.9 %project.1 = bf16[2,4,8,256,128]{4,3,2,1,0:T(8,128)(2,1)} custom-call(bf16[2,4,6,256,128]{4,3,2,1,0:T(8,128)(2,1)} %get-tuple-element.48.first_ref, bf16[2,4,2,256,128]{4,3,2,1,0:T(8,128)(2,1)} %get-tuple-element.49.second_ref, bf16[4,8,128,128]{3,2,1,0:T(8,128)(2,1)} %bitcast.8), custom_call_target="tpu_custom_call" | custom-call | flops 536870912 | bytes 9437184 | tf_op jit(solution)/shard_map/project/pallas_call | solution.py:210
  90.5 6.1 %all-to-all-done.parts_ref = bf16[8,128,128]{2,1,0:T(8,128)(2,1)S(1)} async-done(((bf16[8,128,128]{2,1,0:T(8,128)(2,1)}), bf16[8,128,128]{2,1,0:T(8,128)(2,1)S(1)}, u32[]{:S(2)}, u32[]{:S(2)}) %all-to-all-start) | async-done | bytes 262176 | tf_op jit(solution)/shard_map/all_to_all | solution.py:284
  96.6 0.8 finish.1
Async XLA Ops:
  0.6 51.1 %copy-start = (bf16[32,128,128]{2,1,0:T(8,128)(2,1)S(1)}, bf16[32,128,128]{2,1,0:T(8,128)(2,1)}, u32[]{:S(2)}) copy-start(bf16[32,128,128]{2,1,0:T(8,128)(2,1)} %param.11) | copy-start | bytes 3145732
  0.6 51.1 %copy-start.1 = (s32[32]{0:T(128)S(1)}, s32[32]{0:T(128)}, u32[]{:S(2)}) copy-start(s32[32]{0:T(128)} %counts_ref.3) | copy-start | bytes 388
  7.3 13.7 %collective-permute-start = (bf16[32,48,128]{2,1,0:T(8,128)(2,1)S(1)}, bf16[32,48,128]{2,1,0:T(8,128)(2,1)S(1)}, u32[]{:S(2)}, u32[]{:S(2)}) collective-permute-start(bf16[32,48,128]{2,1,0:T(8,128)(2,1)S(1)} %get-tuple-element.28), channel_id=1, source_target_pairs={{0,4},{1,5},{2,6},{3,7},{4,0},{5,1},{6,2},{7,3},{8,12},{9,13},{10,... | collective-permute-start | bytes 1179656 | tf_op jit(solution)/shard_map/ppermute | solution.py:257
  10.4 18.0 %collective-permute-start.1 = (bf16[32,48,128]{2,1,0:T(8,128)(2,1)S(1)}, bf16[32,48,128]{2,1,0:T(8,128)(2,1)S(1)}, u32[]{:S(2)}, u32[]{:S(2)}) collective-permute-start(bf16[32,48,128]{2,1,0:T(8,128)(2,1)S(1)} %get-tuple-element.29), channel_id=1, source_target_pairs={{0,5},{1,4},{2,7},{3,6},{4,1},{5,0},{6,3},{7,2},{8,13},{9,12},{10,... | collective-permute-start | bytes 1179656 | tf_op jit(solution)/shard_map/ppermute | solution.py:257
  10.4 30.3 %collective-permute-start.4 = (bf16[32,64,128]{2,1,0:T(8,128)(2,1)S(1)}, bf16[32,64,128]{2,1,0:T(8,128)(2,1)S(1)}, u32[]{:S(2)}, u32[]{:S(2)}) collective-permute-start(bf16[32,64,128]{2,1,0:T(8,128)(2,1)S(1)} %get-tuple-element.32), channel_id=1, source_target_pairs={{0,2},{1,3},{2,0},{3,1},{4,6},{5,7},{6,4},{7,5},{8,10},{9,11},{10,... | collective-permute-start | bytes 1572872 | tf_op jit(solution)/shard_map/ppermute | solution.py:257
  11.6 31.1 %collective-permute-start.5 = (bf16[32,64,128]{2,1,0:T(8,128)(2,1)S(1)}, bf16[32,64,128]{2,1,0:T(8,128)(2,1)S(1)}, u32[]{:S(2)}, u32[]{:S(2)}) collective-permute-start(bf16[32,64,128]{2,1,0:T(8,128)(2,1)S(1)} %get-tuple-element.33), channel_id=1, source_target_pairs={{0,6},{1,7},{2,4},{3,5},{4,2},{5,3},{6,0},{7,1},{8,14},{9,15},{10,... | collective-permute-start | bytes 1572872 | tf_op jit(solution)/shard_map/ppermute | solution.py:257
  13.7 37.2 %collective-permute-start.6 = (bf16[32,64,128]{2,1,0:T(8,128)(2,1)S(1)}, bf16[32,64,128]{2,1,0:T(8,128)(2,1)S(1)}, u32[]{:S(2)}, u32[]{:S(2)}) collective-permute-start(bf16[32,64,128]{2,1,0:T(8,128)(2,1)S(1)} %get-tuple-element.34), channel_id=1, source_target_pairs={{0,3},{1,2},{2,1},{3,0},{4,7},{5,6},{6,5},{7,4},{8,11},{9,10},{10,... | collective-permute-start | bytes 1572872 | tf_op jit(solution)/shard_map/ppermute | solution.py:257
  21.0 30.7 %collective-permute-start.7 = (bf16[32,64,128]{2,1,0:T(8,128)(2,1)S(1)}, bf16[32,64,128]{2,1,0:T(8,128)(2,1)S(1)}, u32[]{:S(2)}, u32[]{:S(2)}) collective-permute-start(bf16[32,64,128]{2,1,0:T(8,128)(2,1)S(1)} %get-tuple-element.35), channel_id=1, source_target_pairs={{0,7},{1,6},{2,5},{3,4},{4,3},{5,2},{6,1},{7,0},{8,15},{9,14},{10,... | collective-permute-start | bytes 1572872 | tf_op jit(solution)/shard_map/ppermute | solution.py:257
  28.4 23.3 %collective-permute-start.8 = (bf16[32,64,128]{2,1,0:T(8,128)(2,1)S(1)}, bf16[32,64,128]{2,1,0:T(8,128)(2,1)S(1)}, u32[]{:S(2)}, u32[]{:S(2)}) collective-permute-start(bf16[32,64,128]{2,1,0:T(8,128)(2,1)S(1)} %get-tuple-element.36), channel_id=1, source_target_pairs={{0,1},{1,0},{2,3},{3,2},{4,5},{5,4},{6,7},{7,6},{8,9},{9,8},{10,11... | collective-permute-start | bytes 1572872 | tf_op jit(solution)/shard_map/ppermute | solution.py:257
  40.7 16.3 %collective-permute-start.2 = (bf16[32,16,128]{2,1,0:T(8,128)(2,1)S(1)}, bf16[32,16,128]{2,1,0:T(8,128)(2,1)S(1)}, u32[]{:S(2)}, u32[]{:S(2)}) collective-permute-start(bf16[32,16,128]{2,1,0:T(8,128)(2,1)S(1)} %get-tuple-element.30), channel_id=1, source_target_pairs={{0,4},{1,5},{2,6},{3,7},{4,0},{5,1},{6,2},{7,3},{8,12},{9,13},{10,... | collective-permute-start | bytes 393224 | tf_op jit(solution)/shard_map/ppermute | solution.py:257
  42.7 14.3 %collective-permute-start.3 = (bf16[32,16,128]{2,1,0:T(8,128)(2,1)S(1)}, bf16[32,16,128]{2,1,0:T(8,128)(2,1)S(1)}, u32[]{:S(2)}, u32[]{:S(2)}) collective-permute-start(bf16[32,16,128]{2,1,0:T(8,128)(2,1)S(1)} %get-tuple-element.31), channel_id=1, source_target_pairs={{0,5},{1,4},{2,7},{3,6},{4,1},{5,0},{6,3},{7,2},{8,13},{9,12},{10,... | collective-permute-start | bytes 393224 | tf_op jit(solution)/shard_map/ppermute | solution.py:257
  59.6 10.7 %collective-permute-start.9 = (bf16[8,128,128]{2,1,0:T(8,128)(2,1)S(1)}, bf16[8,128,128]{2,1,0:T(8,128)(2,1)S(1)}, u32[]{:S(2)}, u32[]{:S(2)}) collective-permute-start(bf16[8,128,128]{2,1,0:T(8,128)(2,1)S(1)} %get-tuple-element.45), channel_id=1, source_target_pairs={{0,128},{8,136},{16,144},{24,152},{32,160},{40,168},{48,176},{56,1... | collective-permute-start | bytes 786440 | tf_op jit(solution)/shard_map/ppermute | solution.py:263
  60.8 13.3 %collective-permute-start.10 = (bf16[8,128,128]{2,1,0:T(8,128)(2,1)S(1)}, bf16[8,128,128]{2,1,0:T(8,128)(2,1)S(1)}, u32[]{:S(2)}, u32[]{:S(2)}) collective-permute-start(bf16[8,128,128]{2,1,0:T(8,128)(2,1)S(1)} %get-tuple-element.46), channel_id=1, source_target_pairs={{0,64},{8,72},{16,80},{24,88},{32,96},{40,104},{48,112},{56,120},{... | collective-permute-start | bytes 786440 | tf_op jit(solution)/shard_map/ppermute | solution.py:263
  62.2 13.1 %collective-permute-start.11 = (bf16[8,128,128]{2,1,0:T(8,128)(2,1)S(1)}, bf16[8,128,128]{2,1,0:T(8,128)(2,1)S(1)}, u32[]{:S(2)}, u32[]{:S(2)}) collective-permute-start(bf16[8,128,128]{2,1,0:T(8,128)(2,1)S(1)} %get-tuple-element.47), channel_id=1, source_target_pairs={{0,192},{8,200},{16,208},{24,216},{32,224},{40,232},{48,240},{56,2... | collective-permute-start | bytes 786440 | tf_op jit(solution)/shard_map/ppermute | solution.py:263
  76.1 20.5 %all-to-all-start = ((bf16[8,128,128]{2,1,0:T(8,128)(2,1)}), bf16[8,128,128]{2,1,0:T(8,128)(2,1)S(1)}, u32[]{:S(2)}, u32[]{:S(2)}) async-start(bf16[8,128,128]{2,1,0:T(8,128)(2,1)} %join.1), calls=%async_computation | async-start | bytes 524288 | tf_op jit(solution)/shard_map/all_to_all | solution.py:284

commit v4 on v3

--- a/solution.py
+++ b/solution.py
@@ -280,6 +280,7 @@
         compiler_params=pltpu.CompilerParams(vmem_limit_bytes=8 << 20),
         name="join",
     )(covs[0], *to_y(covs))
+    parts, projected = lax.optimization_barrier((parts, projected))
     rings = [[y * NZ + z for z in range(NZ)] for y in range(NY)]
     parts = lax.all_to_all(parts, "dp", 0, 0, axis_index_groups=rings, tiled=True)
     covariance = pl.pallas_call(

time: 97.7 us -> 96.7 us (0.990)
  blocking collectives: 0 us -> 20.3 us
  waiting for transfers between devices: 52.2 us -> 40.2 us
  starting transfers between devices: 22.4 us -> 14 us
    all_to_all x0 -> x1, blocking collectives: none -> 20.3 us  [body(): lax.all_to_all(parts, 'dp', 0, 0, axis_index_groups=rings, tiled=True)]
    all_to_all x1 -> x0, starting transfers between devices: 8.46 us -> none  [body(): lax.all_to_all(parts, 'dp', 0, 0, axis_index_groups=rings, tiled=True)]
    all_to_all x1 -> x0, waiting for transfers between devices: 6.13 us -> none  [body(): lax.all_to_all(parts, 'dp', 0, 0, axis_index_groups=rings, tiled=True)]
    ppermute x3, waiting for transfers between devices: 11.6 us -> 5.68 us  [to_y(): lax.ppermute(covs[dy], 'dp', [(i, i ^ dy * NZ) for i in range(NY * NZ)])]
  transfers between devices with their start and end apart: 13 -> 12, of which waited for: 9 -> 8; matrix products, arithmetic and copies ran while one was open for 0% -> 0% of each run, Pallas kernels for 12% -> 12%
where the time goes in v4:
time: 96.7 us; the launch traced here: 96.5 us
  waiting for transfers between devices  40.2 us (42%)
  Pallas kernels  21.4 us (22%)
  blocking collectives  20.3 us (21%)
  starting transfers between devices  14 us (14%)
    ppermute x9, waiting for transfers between devices, exchange(): lax.ppermute(piece, 'order', [(i, i ^ d) for i in range(NO)])  34.5 us
    all_to_all x1, blocking collectives, body(): lax.all_to_all(parts, 'dp', 0, 0, axis_index_groups=rings, tiled=True)  20.3 us
    ppermute x9, starting transfers between devices, exchange(): lax.ppermute(piece, 'order', [(i, i ^ d) for i in range(NO)])  9.88 us
    pallas_call x2, Pallas kernels, slots(): pl.pallas_call(functools.partial(slot_kernel, scale, start, len(covs)), g...  7.91 us
    pallas_call x1, Pallas kernels, spectra(): pl.pallas_call(spectrum_kernel, grid=(count // step,), in_specs=[pl.Block...  6.64 us
    pallas_call x1, Pallas kernels, project(): pl.pallas_call(project_kernel, grid=(GROUPS,), in_specs=[pl.BlockSpec(hel...  5.91 us
    ppermute x3, waiting for transfers between devices, to_y(): lax.ppermute(covs[dy], 'dp', [(i, i ^ dy * NZ) for i in range(NY * NZ)])  5.68 us
    ppermute x3, starting transfers between devices, to_y(): lax.ppermute(covs[dy], 'dp', [(i, i ^ dy * NZ) for i in range(NY * NZ)])  4.09 us
  transfers between devices with their start and end apart: 12, of which 8 were waited for; matrix products, arithmetic and copies ran while one was open for 0% of the time, Pallas kernels for 12%

profile of v4, /device:TPU:24, one launch (start us, length us, event | category | flops | bytes accessed | tf_op | source)
XLA Modules:
  0.0 96.5 jit_solution(17453848882062425914)
XLA Ops:
  0.6 0.0 copy-start
  0.6 0.0 copy-start.1
  0.7 6.6 %spectra.1 = (bf16[32,48,128]{2,1,0:T(8,128)(2,1)S(1)}, bf16[32,48,128]{2,1,0:T(8,128)(2,1)S(1)}, bf16[32,64,128]{2,1,0:T(8,128)(2,1)S(1)}, bf16[32,64,128]{2,1,...) custom-call(bf16[32,128,512]{2,1,0:T(8,128)(2,1)} %x_ref.1, ...), custom_call_target="tpu_custom_call" | custom-call | flops 2684354560 | bytes 8388608 | tf_op jit(solution)/shard_map/spectra/pallas_call | solution.py:91
  7.3 3.1 %collective-permute-start = (bf16[32,48,128]{2,1,0:T(8,128)(2,1)S(1)}, bf16[32,48,128]{2,1,0:T(8,128)(2,1)S(1)}, u32[]{:S(2)}, u32[]{:S(2)}) collective-permute-start(bf16[32,48,128]{2,1,0:T(8,128)(2,1)S(1)} %get-tuple-element.30), channel_id=1, source_target_pairs={{0,4},{1,5},{2,6},{3,7},{4,0},{5,1},{6,2},{7,3},{8,12},{9,13},{10,... | collective-permute-start | bytes 1179656 | tf_op jit(solution)/shard_map/ppermute | solution.py:257
  10.4 0.0 collective-permute-start.1
  10.4 1.2 %collective-permute-start.4 = (bf16[32,64,128]{2,1,0:T(8,128)(2,1)S(1)}, bf16[32,64,128]{2,1,0:T(8,128)(2,1)S(1)}, u32[]{:S(2)}, u32[]{:S(2)}) collective-permute-start(bf16[32,64,128]{2,1,0:T(8,128)(2,1)S(1)} %get-tuple-element.34), channel_id=1, source_target_pairs={{0,2},{1,3},{2,0},{3,1},{4,6},{5,7},{6,4},{7,5},{8,10},{9,11},{10,... | collective-permute-start | bytes 1572872 | tf_op jit(solution)/shard_map/ppermute | solution.py:257
  11.6 2.1 %collective-permute-start.5 = (bf16[32,64,128]{2,1,0:T(8,128)(2,1)S(1)}, bf16[32,64,128]{2,1,0:T(8,128)(2,1)S(1)}, u32[]{:S(2)}, u32[]{:S(2)}) collective-permute-start(bf16[32,64,128]{2,1,0:T(8,128)(2,1)S(1)} %get-tuple-element.35), channel_id=1, source_target_pairs={{0,6},{1,7},{2,4},{3,5},{4,2},{5,3},{6,0},{7,1},{8,14},{9,15},{10,... | collective-permute-start | bytes 1572872 | tf_op jit(solution)/shard_map/ppermute | solution.py:257
  13.7 0.6 collective-permute-start.6
  14.3 6.7 %collective-permute-done.refs_0_ = bf16[32,48,128]{2,1,0:T(8,128)(2,1)S(1)} collective-permute-done((bf16[32,48,128]{2,1,0:T(8,128)(2,1)S(1)}, bf16[32,48,128]{2,1,0:T(8,128)(2,1)S(1)}, u32[]{:S(2)}, u32[]{:S(2)}) %collective-permute-start) | collective-permute-done | bytes 393248 | tf_op jit(solution)/shard_map/ppermute | solution.py:257
  21.0 0.1 collective-permute-start.7
  21.1 7.3 %collective-permute-done.1.refs_1_ = bf16[32,48,128]{2,1,0:T(8,128)(2,1)S(1)} collective-permute-done((bf16[32,48,128]{2,1,0:T(8,128)(2,1)S(1)}, bf16[32,48,128]{2,1,0:T(8,128)(2,1)S(1)}, u32[]{:S(2)}, u32[]{:S(2)}) %collective-permute-start.1) | collective-permute-done | bytes 393248 | tf_op jit(solution)/shard_map/ppermute | solution.py:257
  28.4 0.8 collective-permute-start.8
  29.2 11.5 %collective-permute-done.4.refs_2_ = bf16[32,64,128]{2,1,0:T(8,128)(2,1)S(1)} collective-permute-done((bf16[32,64,128]{2,1,0:T(8,128)(2,1)S(1)}, bf16[32,64,128]{2,1,0:T(8,128)(2,1)S(1)}, u32[]{:S(2)}, u32[]{:S(2)}) %collective-permute-start.4) | collective-permute-done | bytes 524320 | tf_op jit(solution)/shard_map/ppermute | solution.py:257
  40.7 2.0 %collective-permute-start.2 = (bf16[32,16,128]{2,1,0:T(8,128)(2,1)S(1)}, bf16[32,16,128]{2,1,0:T(8,128)(2,1)S(1)}, u32[]{:S(2)}, u32[]{:S(2)}) collective-permute-start(bf16[32,16,128]{2,1,0:T(8,128)(2,1)S(1)} %get-tuple-element.32), channel_id=1, source_target_pairs={{0,4},{1,5},{2,6},{3,7},{4,0},{5,1},{6,2},{7,3},{8,12},{9,13},{10,... | collective-permute-start | bytes 393224 | tf_op jit(solution)/shard_map/ppermute | solution.py:257
  42.7 0.0 collective-permute-done.5.refs_3_
  42.7 0.0 collective-permute-start.3
  42.7 8.2 %collective-permute-done.6.refs_4_ = bf16[32,64,128]{2,1,0:T(8,128)(2,1)S(1)} collective-permute-done((bf16[32,64,128]{2,1,0:T(8,128)(2,1)S(1)}, bf16[32,64,128]{2,1,0:T(8,128)(2,1)S(1)}, u32[]{:S(2)}, u32[]{:S(2)}) %collective-permute-start.6) | collective-permute-done | bytes 524320 | tf_op jit(solution)/shard_map/ppermute | solution.py:257
  50.9 0.8 collective-permute-done.7.refs_5_
  51.7 0.0 collective-permute-done.8.refs_6_
  51.7 0.0 copy-done
  51.7 0.0 copy-done.1
  51.7 5.3 %slots.2 = (bf16[2,4,6,256,128]{4,3,2,1,0:T(8,128)(2,1)}, bf16[8,128,128]{2,1,0:T(8,128)(2,1)S(1)}, bf16[8,128,128]{2,1,0:T(8,128)(2,1)S(1)}, bf16[8,128,128]{2,1,0:T(8,128)(2,1)S(1)}, bf16[8,128,128]{2,1,0:T(8,128)(2,1)S(1)}) custom-call(s32[32]{0:T(128)S(1)} %copy-done.1, bf16[32,48,128]{2,1,0:T(8,128)(2,1)S(1)} %collective-permute-done.refs_0_, ...), custom_call_target="tpu_custom_call" | custom-call | flops 4831838208 | bytes 9437184 | tf_op jit(solution)/shard_map/slots/pallas_call | solution.py:160
  57.0 0.0 collective-permute-done.2.refs_0_
  57.0 0.0 collective-permute-done.3.refs_1_
  57.0 2.6 %slots.3 = (bf16[2,4,2,256,128]{4,3,2,1,0:T(8,128)(2,1)}, bf16[8,128,128]{2,1,0:T(8,128)(2,1)S(1)}, bf16[8,128,128]{2,1,0:T(8,128)(2,1)S(1)}, bf16[8,128,128]{2,1,0:T(8,128)(2,1)S(1)}, bf16[8,128,128]{2,1,0:T(8,128)(2,1)S(1)}) custom-call(s32[32]{0:T(128)S(1)} %copy-done.1, ...), custom_call_target="tpu_custom_call", output_to_operand_aliasing={{1}: (10, {}), {2}: (11, {}), {3}: (12, {}), {4}: (13, {})} | custom-call | flops 1610612736 | bytes 3145728 | tf_op jit(solution)/shard_map/slots/pallas_call | solution.py:160
  59.6 1.2 %collective-permute-start.9 = (bf16[8,128,128]{2,1,0:T(8,128)(2,1)S(1)}, bf16[8,128,128]{2,1,0:T(8,128)(2,1)S(1)}, u32[]{:S(2)}, u32[]{:S(2)}) collective-permute-start(bf16[8,128,128]{2,1,0:T(8,128)(2,1)S(1)} %get-tuple-element.47), channel_id=1, source_target_pairs={{0,128},{8,136},{16,144},{24,152},{32,160},{40,168},{48,176},{56,1... | collective-permute-start | bytes 786440 | tf_op jit(solution)/shard_map/ppermute | solution.py:263
  60.9 1.4 %collective-permute-start.10 = (bf16[8,128,128]{2,1,0:T(8,128)(2,1)S(1)}, bf16[8,128,128]{2,1,0:T(8,128)(2,1)S(1)}, u32[]{:S(2)}, u32[]{:S(2)}) collective-permute-start(bf16[8,128,128]{2,1,0:T(8,128)(2,1)S(1)} %get-tuple-element.48), channel_id=1, source_target_pairs={{0,64},{8,72},{16,80},{24,88},{32,96},{40,104},{48,112},{56,120},{... | collective-permute-start | bytes 786440 | tf_op jit(solution)/shard_map/ppermute | solution.py:263
  62.2 1.5 %collective-permute-start.11 = (bf16[8,128,128]{2,1,0:T(8,128)(2,1)S(1)}, bf16[8,128,128]{2,1,0:T(8,128)(2,1)S(1)}, u32[]{:S(2)}, u32[]{:S(2)}) collective-permute-start(bf16[8,128,128]{2,1,0:T(8,128)(2,1)S(1)} %get-tuple-element.49), channel_id=1, source_target_pairs={{0,192},{8,200},{16,208},{24,216},{32,224},{40,232},{48,240},{56,2... | collective-permute-start | bytes 786440 | tf_op jit(solution)/shard_map/ppermute | solution.py:263
  63.7 5.9 %project.1 = bf16[2,4,8,256,128]{4,3,2,1,0:T(8,128)(2,1)} custom-call(bf16[2,4,6,256,128]{4,3,2,1,0:T(8,128)(2,1)} %get-tuple-element.50.first_ref, bf16[2,4,2,256,128]{4,3,2,1,0:T(8,128)(2,1)} %get-tuple-element.51.second_ref, bf16[4,8,128,128]{3,2,1,0:T(8,128)(2,1)} %bitcast.8), custom_call_target="tpu_custom_call" | custom-call | flops 536870912 | bytes 9437184 | tf_op jit(solution)/shard_map/project/pallas_call | solution.py:210
  69.6 0.7 collective-permute-done.9.refs_1_
  70.3 3.9 %collective-permute-done.10.refs_2_ = bf16[8,128,128]{2,1,0:T(8,128)(2,1)S(1)} collective-permute-done((bf16[8,128,128]{2,1,0:T(8,128)(2,1)S(1)}, bf16[8,128,128]{2,1,0:T(8,128)(2,1)S(1)}, u32[]{:S(2)}, u32[]{:S(2)}) %collective-permute-start.10) | collective-permute-done | bytes 262176 | tf_op jit(solution)/shard_map/ppermute | solution.py:263
  74.2 1.1 %collective-permute-done.11.refs_3_ = bf16[8,128,128]{2,1,0:T(8,128)(2,1)S(1)} collective-permute-done((bf16[8,128,128]{2,1,0:T(8,128)(2,1)S(1)}, bf16[8,128,128]{2,1,0:T(8,128)(2,1)S(1)}, u32[]{:S(2)}, u32[]{:S(2)}) %collective-permute-start.11) | collective-permute-done | bytes 262176 | tf_op jit(solution)/shard_map/ppermute | solution.py:263
  75.3 0.1 join.1
  75.4 20.3 %all_to_all.5.parts_ref = bf16[8,128,128]{2,1,0:T(8,128)(2,1)S(1)} all-to-all(bf16[8,128,128]{2,1,0:T(8,128)(2,1)S(1)} %join.1), channel_id=1, replica_groups={{0,8,16,24,32,40,48,56},{64,72,80,88,96,104,112,120},{128,136,144,152,1..., dimensions={0} | all-to-all | bytes 524288 | tf_op jit(solution)/shard_map/all_to_all | solution.py:285
  95.8 0.8 finish.1
Async XLA Ops:
  0.6 51.1 %copy-start = (bf16[32,128,128]{2,1,0:T(8,128)(2,1)S(1)}, bf16[32,128,128]{2,1,0:T(8,128)(2,1)}, u32[]{:S(2)}) copy-start(bf16[32,128,128]{2,1,0:T(8,128)(2,1)} %param.11) | copy-start | bytes 3145732
  0.6 51.1 %copy-start.1 = (s32[32]{0:T(128)S(1)}, s32[32]{0:T(128)}, u32[]{:S(2)}) copy-start(s32[32]{0:T(128)} %counts_ref.3) | copy-start | bytes 388
  7.3 13.7 %collective-permute-start = (bf16[32,48,128]{2,1,0:T(8,128)(2,1)S(1)}, bf16[32,48,128]{2,1,0:T(8,128)(2,1)S(1)}, u32[]{:S(2)}, u32[]{:S(2)}) collective-permute-start(bf16[32,48,128]{2,1,0:T(8,128)(2,1)S(1)} %get-tuple-element.30), channel_id=1, source_target_pairs={{0,4},{1,5},{2,6},{3,7},{4,0},{5,1},{6,2},{7,3},{8,12},{9,13},{10,... | collective-permute-start | bytes 1179656 | tf_op jit(solution)/shard_map/ppermute | solution.py:257
  10.4 18.0 %collective-permute-start.1 = (bf16[32,48,128]{2,1,0:T(8,128)(2,1)S(1)}, bf16[32,48,128]{2,1,0:T(8,128)(2,1)S(1)}, u32[]{:S(2)}, u32[]{:S(2)}) collective-permute-start(bf16[32,48,128]{2,1,0:T(8,128)(2,1)S(1)} %get-tuple-element.31), channel_id=1, source_target_pairs={{0,5},{1,4},{2,7},{3,6},{4,1},{5,0},{6,3},{7,2},{8,13},{9,12},{10,... | collective-permute-start | bytes 1179656 | tf_op jit(solution)/shard_map/ppermute | solution.py:257
  10.4 30.3 %collective-permute-start.4 = (bf16[32,64,128]{2,1,0:T(8,128)(2,1)S(1)}, bf16[32,64,128]{2,1,0:T(8,128)(2,1)S(1)}, u32[]{:S(2)}, u32[]{:S(2)}) collective-permute-start(bf16[32,64,128]{2,1,0:T(8,128)(2,1)S(1)} %get-tuple-element.34), channel_id=1, source_target_pairs={{0,2},{1,3},{2,0},{3,1},{4,6},{5,7},{6,4},{7,5},{8,10},{9,11},{10,... | collective-permute-start | bytes 1572872 | tf_op jit(solution)/shard_map/ppermute | solution.py:257
  11.6 31.1 %collective-permute-start.5 = (bf16[32,64,128]{2,1,0:T(8,128)(2,1)S(1)}, bf16[32,64,128]{2,1,0:T(8,128)(2,1)S(1)}, u32[]{:S(2)}, u32[]{:S(2)}) collective-permute-start(bf16[32,64,128]{2,1,0:T(8,128)(2,1)S(1)} %get-tuple-element.35), channel_id=1, source_target_pairs={{0,6},{1,7},{2,4},{3,5},{4,2},{5,3},{6,0},{7,1},{8,14},{9,15},{10,... | collective-permute-start | bytes 1572872 | tf_op jit(solution)/shard_map/ppermute | solution.py:257
  13.7 37.2 %collective-permute-start.6 = (bf16[32,64,128]{2,1,0:T(8,128)(2,1)S(1)}, bf16[32,64,128]{2,1,0:T(8,128)(2,1)S(1)}, u32[]{:S(2)}, u32[]{:S(2)}) collective-permute-start(bf16[32,64,128]{2,1,0:T(8,128)(2,1)S(1)} %get-tuple-element.36), channel_id=1, source_target_pairs={{0,3},{1,2},{2,1},{3,0},{4,7},{5,6},{6,5},{7,4},{8,11},{9,10},{10,... | collective-permute-start | bytes 1572872 | tf_op jit(solution)/shard_map/ppermute | solution.py:257
  21.0 30.7 %collective-permute-start.7 = (bf16[32,64,128]{2,1,0:T(8,128)(2,1)S(1)}, bf16[32,64,128]{2,1,0:T(8,128)(2,1)S(1)}, u32[]{:S(2)}, u32[]{:S(2)}) collective-permute-start(bf16[32,64,128]{2,1,0:T(8,128)(2,1)S(1)} %get-tuple-element.37), channel_id=1, source_target_pairs={{0,7},{1,6},{2,5},{3,4},{4,3},{5,2},{6,1},{7,0},{8,15},{9,14},{10,... | collective-permute-start | bytes 1572872 | tf_op jit(solution)/shard_map/ppermute | solution.py:257
  28.4 23.3 %collective-permute-start.8 = (bf16[32,64,128]{2,1,0:T(8,128)(2,1)S(1)}, bf16[32,64,128]{2,1,0:T(8,128)(2,1)S(1)}, u32[]{:S(2)}, u32[]{:S(2)}) collective-permute-start(bf16[32,64,128]{2,1,0:T(8,128)(2,1)S(1)} %get-tuple-element.38), channel_id=1, source_target_pairs={{0,1},{1,0},{2,3},{3,2},{4,5},{5,4},{6,7},{7,6},{8,9},{9,8},{10,11... | collective-permute-start | bytes 1572872 | tf_op jit(solution)/shard_map/ppermute | solution.py:257
  40.7 16.3 %collective-permute-start.2 = (bf16[32,16,128]{2,1,0:T(8,128)(2,1)S(1)}, bf16[32,16,128]{2,1,0:T(8,128)(2,1)S(1)}, u32[]{:S(2)}, u32[]{:S(2)}) collective-permute-start(bf16[32,16,128]{2,1,0:T(8,128)(2,1)S(1)} %get-tuple-element.32), channel_id=1, source_target_pairs={{0,4},{1,5},{2,6},{3,7},{4,0},{5,1},{6,2},{7,3},{8,12},{9,13},{10,... | collective-permute-start | bytes 393224 | tf_op jit(solution)/shard_map/ppermute | solution.py:257
  42.7 14.3 %collective-permute-start.3 = (bf16[32,16,128]{2,1,0:T(8,128)(2,1)S(1)}, bf16[32,16,128]{2,1,0:T(8,128)(2,1)S(1)}, u32[]{:S(2)}, u32[]{:S(2)}) collective-permute-start(bf16[32,16,128]{2,1,0:T(8,128)(2,1)S(1)} %get-tuple-element.33), channel_id=1, source_target_pairs={{0,5},{1,4},{2,7},{3,6},{4,1},{5,0},{6,3},{7,2},{8,13},{9,12},{10,... | collective-permute-start | bytes 393224 | tf_op jit(solution)/shard_map/ppermute | solution.py:257
  59.6 10.7 %collective-permute-start.9 = (bf16[8,128,128]{2,1,0:T(8,128)(2,1)S(1)}, bf16[8,128,128]{2,1,0:T(8,128)(2,1)S(1)}, u32[]{:S(2)}, u32[]{:S(2)}) collective-permute-start(bf16[8,128,128]{2,1,0:T(8,128)(2,1)S(1)} %get-tuple-element.47), channel_id=1, source_target_pairs={{0,128},{8,136},{16,144},{24,152},{32,160},{40,168},{48,176},{56,1... | collective-permute-start | bytes 786440 | tf_op jit(solution)/shard_map/ppermute | solution.py:263
  60.9 13.3 %collective-permute-start.10 = (bf16[8,128,128]{2,1,0:T(8,128)(2,1)S(1)}, bf16[8,128,128]{2,1,0:T(8,128)(2,1)S(1)}, u32[]{:S(2)}, u32[]{:S(2)}) collective-permute-start(bf16[8,128,128]{2,1,0:T(8,128)(2,1)S(1)} %get-tuple-element.48), channel_id=1, source_target_pairs={{0,64},{8,72},{16,80},{24,88},{32,96},{40,104},{48,112},{56,120},{... | collective-permute-start | bytes 786440 | tf_op jit(solution)/shard_map/ppermute | solution.py:263
  62.2 13.1 %collective-permute-start.11 = (bf16[8,128,128]{2,1,0:T(8,128)(2,1)S(1)}, bf16[8,128,128]{2,1,0:T(8,128)(2,1)S(1)}, u32[]{:S(2)}, u32[]{:S(2)}) collective-permute-start(bf16[8,128,128]{2,1,0:T(8,128)(2,1)S(1)} %get-tuple-element.49), channel_id=1, source_target_pairs={{0,192},{8,200},{16,208},{24,216},{32,224},{40,232},{48,240},{56,2... | collective-permute-start | bytes 786440 | tf_op jit(solution)/shard_map/ppermute | solution.py:263
